TPU v7x, 256 devices: a whole 4x4x8 slice. The times are simulated.
256 devices in a mesh: seq: 32 (over y, x, core), chan: 8 (over z).
Axes of the slice: x: 4, y: 4, z: 8, core: 2. Of those that a mesh axis runs over, the one named last changes fastest.
Arguments:
- conv_in: bfloat16 [32, 512, 512], P(None, 'seq', 'chan'), may hold values from -4 to 4
- conv_gate: bfloat16 [32, 512, 512], P(None, 'seq', 'chan'), may hold values from -4 to 4
- long_filter: float32 [32, 512, 512], P(None, 'seq', 'chan'), may hold values from -1.1 to 1.1
- skip_gain: float32 [512], P('chan'), may hold values from 0.5 to 1.5
- queries: bfloat16 [32, 512, 1024], P(None, 'seq', 'chan'), may hold values from -40 to 40
- keys_in: bfloat16 [32, 512, 1024], P(None, 'seq', 'chan'), may hold values from -40 to 40
- w_value: bfloat16 [512, 1024], P(None, 'chan'), may hold values from -0.25 to 0.25
Outputs:
- conv_out: bfloat16 [32, 512, 512], P(None, 'seq', 'chan')
- attended: bfloat16 [32, 512, 1024], P(None, 'seq', 'chan')
All inputs are finite; a program needn't handle non-finite values.
Results may differ from a plain program's by a relative error of at most 0.015.
Values may be sent and summed in bfloat16 or wider, within the bound.
A program may use at most 64 MiB of HBM per device.

v0:
```python
import math

import jax
import jax.numpy as jnp
from jax import lax
from jax.sharding import PartitionSpec as P


def mixdot(form, left, right):
    return jnp.einsum(form, left, right, precision=lax.Precision.HIGHEST)


def channel_convolve(signal, long_filter):
    moved_sig, moved_tap = (
        lax.all_to_all(
            signal.astype(jnp.bfloat16), "seq", split_axis=2, concat_axis=1, tiled=True
        ).astype(signal.dtype),
        lax.all_to_all(
            long_filter.astype(jnp.bfloat16), "seq", split_axis=2, concat_axis=1, tiled=True
        ).astype(long_filter.dtype),
    )
    blocks = moved_sig.shape[0]
    length_q = moved_sig.shape[1]
    length_p = 2 * blocks
    total = length_p * length_q
    both = jnp.concatenate([moved_sig, moved_tap], axis=2).transpose(2, 0, 1)
    iota_p = jnp.arange(length_p, dtype=jnp.int32)
    iota_r = jnp.arange(blocks, dtype=jnp.int32)
    iota_q = jnp.arange(length_q, dtype=jnp.int32)
    ang_p = (iota_p[:, None] * iota_r[None, :] % length_p).astype(jnp.float32) * (
        2.0 * math.pi / length_p
    )
    ang_q = (iota_q[:, None] * iota_q[None, :] % length_q).astype(jnp.float32) * (
        2.0 * math.pi / length_q
    )
    ang_t = (iota_p[:, None] * iota_q[None, :] % total).astype(jnp.float32) * (
        2.0 * math.pi / total
    )
    cos_p = jnp.cos(ang_p)
    sin_p = jnp.sin(ang_p)
    cos_q = jnp.cos(ang_q)
    sin_q = jnp.sin(ang_q)
    cos_t = jnp.cos(ang_t)
    sin_t = jnp.sin(ang_t)
    first_re = mixdot("kn,cnq->ckq", cos_p, both)
    first_im = -mixdot("kn,cnq->ckq", sin_p, both)
    tw_re = first_re * cos_t + first_im * sin_t
    tw_im = first_im * cos_t - first_re * sin_t
    spec_re = mixdot("ckq,qm->ckm", tw_re, cos_q) + mixdot("ckq,qm->ckm", tw_im, sin_q)
    spec_im = mixdot("ckq,qm->ckm", tw_im, cos_q) - mixdot("ckq,qm->ckm", tw_re, sin_q)
    half_count = both.shape[0] // 2
    sig_re = spec_re[:half_count]
    sig_im = spec_im[:half_count]
    tap_re = spec_re[half_count:]
    tap_im = spec_im[half_count:]
    prod_re = sig_re * tap_re - sig_im * tap_im
    prod_im = sig_re * tap_im + sig_im * tap_re
    inner_re = mixdot("ckm,mq->ckq", prod_re, cos_q) - mixdot("ckm,mq->ckq", prod_im, sin_q)
    inner_im = mixdot("ckm,mq->ckq", prod_im, cos_q) + mixdot("ckm,mq->ckq", prod_re, sin_q)
    turned_re = inner_re * cos_t - inner_im * sin_t
    turned_im = inner_im * cos_t + inner_re * sin_t
    result = (mixdot("kn,ckq->cnq", cos_p, turned_re) - mixdot("kn,ckq->cnq", sin_p, turned_im)) * (
        1.0 / total
    )
    return lax.all_to_all(
        result.transpose(1, 2, 0).astype(jnp.bfloat16),
        "seq",
        split_axis=1,
        concat_axis=2,
        tiled=True,
    ).astype(jnp.float32)


def body(conv_in, conv_gate, long_filter, skip_gain, queries, keys_in, w_value):
    blocks, slab_rows, channels = conv_in.shape
    my_index = lax.axis_index("seq")
    tokens = blocks * slab_rows
    signal = conv_in.astype(jnp.float32)
    positions = (
        jnp.arange(blocks, dtype=jnp.int32)[:, None] * tokens
        + my_index * slab_rows
        + jnp.arange(slab_rows, dtype=jnp.int32)[None, :]
    )
    convolved = channel_convolve(signal, long_filter)
    mixed = (convolved + skip_gain * signal) * conv_gate.astype(jnp.float32)
    conv_out = mixed.astype(jnp.bfloat16)
    head_size = w_value.shape[1]
    piece = lax.all_gather(conv_out, "chan", axis=2, tiled=True)
    piece_width = piece.shape[2]
    value_sum = jnp.dot(
        piece.reshape(tokens, piece_width), w_value, preferred_element_type=jnp.float32
    )
    values = value_sum.astype(jnp.bfloat16).reshape(blocks, slab_rows, head_size)
    query_rows = queries.reshape(tokens, head_size)
    query_pos = positions.reshape(tokens)
    score_scale = 1.0 / math.sqrt(head_size)
    empty_state = (
        jnp.full((tokens,), -1e30, jnp.float32),
        jnp.zeros((tokens,), jnp.float32),
        jnp.zeros((tokens, head_size), jnp.float32),
    )
    key_piece = lax.all_gather(keys_in, "seq", axis=1, tiled=True)
    value_piece = lax.all_gather(values, "seq", axis=1, tiled=True)
    width_now = key_piece.shape[1]
    target = max(1, 1024 // blocks)
    step_size = 1
    for candidate in range(min(width_now, target), 0, -1):
        step_size = candidate
        break

    def key_step(step_index, current):
        row_best, row_total, row_accum = current
        offset = step_index * step_size
        key_block = lax.dynamic_slice_in_dim(key_piece, offset, step_size, 1).reshape(
            blocks * step_size, head_size
        )
        value_block = lax.dynamic_slice_in_dim(value_piece, offset, step_size, 1).reshape(
            blocks * step_size, head_size
        )
        key_pos = (
            jnp.arange(blocks, dtype=jnp.int32)[:, None] * tokens
            + offset
            + jnp.arange(step_size, dtype=jnp.int32)[None, :]
        ).reshape(blocks * step_size)
        scores = (
            jnp.einsum("qd,kd->qk", query_rows, key_block, preferred_element_type=jnp.float32)
            * score_scale
        )
        allowed = key_pos[None, :] <= query_pos[:, None]
        scores = jnp.where(allowed, scores, -1e30)
        new_best = jnp.maximum(row_best, jnp.max(scores, axis=1))
        factor = jnp.exp(row_best - new_best)
        weights = jnp.where(allowed, jnp.exp(scores - new_best[:, None]), 0.0)
        row_total = row_total * factor + jnp.sum(weights, axis=1)
        row_accum = row_accum * factor[:, None] + jnp.dot(
            weights.astype(jnp.bfloat16), value_block, preferred_element_type=jnp.float32
        )
        return (new_best, row_total, row_accum)

    final_best, final_total, final_accum = lax.fori_loop(
        0, width_now // step_size, key_step, empty_state
    )
    attended = (
        (final_accum / final_total[:, None])
        .astype(jnp.bfloat16)
        .reshape(blocks, slab_rows, head_size)
    )
    return (conv_out, attended)


def solution(mesh):
    return jax.shard_map(
        body,
        mesh=mesh,
        in_specs=(
            P(None, "seq", "chan"),
            P(None, "seq", "chan"),
            P(None, "seq", "chan"),
            P("chan"),
            P(None, "seq", "chan"),
            P(None, "seq", "chan"),
            P(None, "chan"),
        ),
        out_specs=(P(None, "seq", "chan"), P(None, "seq", "chan")),
        check_vma=False,
    )
```

profile of v0, /device:TPU:1, one launch (start us, length us, event | category | flops | bytes accessed | tf_op | source)
XLA Modules:
  0.0 245.0 jit_solution(10891590349229744156)
XLA Ops:
  10.0 8.6 %all-to-all-start.1 = ((bf16[32,2,512]{2,1,0:T(2,128)(2,1)}), bf16[32,2,512]{2,1,0:T(2,128)(2,1)S(1)}, u32[]{:S(2)}, u32[]{:S(2)}) async-start(bf16[32,2,512]{2,1,0:T(2,128)(2,1)} %reshape.130), calls=%async_computation.1 | async-start | bytes 131072 | tf_op jit(solution)/shard_map/all_to_all | solution.py:18
  18.6 1.2 copy.75
  20.7 5.2 %all-to-all-done.1 = bf16[32,2,512]{2,1,0:T(2,128)(2,1)S(1)} async-done(((bf16[32,2,512]{2,1,0:T(2,128)(2,1)}), bf16[32,2,512]{2,1,0:T(2,128)(2,1)S(1)}, u32[]{:S(2)}, u32[]{:S(2)}) %all-to-all-start.1) | async-done | bytes 65568 | tf_op jit(solution)/shard_map/all_to_all | solution.py:18
  26.0 3.9 %all-to-all-start = ((bf16[32,2,512]{2,1,0:T(2,128)(2,1)}), bf16[32,2,512]{2,1,0:T(2,128)(2,1)S(1)}, u32[]{:S(2)}, u32[]{:S(2)}) async-start(bf16[32,2,512]{2,1,0:T(2,128)(2,1)} %reshape.132), calls=%async_computation | async-start | bytes 131072 | tf_op jit(solution)/shard_map/all_to_all | solution.py:15
  30.7 6.6 %all-to-all-done = bf16[32,2,512]{2,1,0:T(2,128)(2,1)S(1)} async-done(((bf16[32,2,512]{2,1,0:T(2,128)(2,1)}), bf16[32,2,512]{2,1,0:T(2,128)(2,1)S(1)}, u32[]{:S(2)}, u32[]{:S(2)}) %all-to-all-start) | async-done | bytes 65568 | tf_op jit(solution)/shard_map/all_to_all | solution.py:15
  38.7 5.4 %fusion.30 = f32[4,64,512]{2,1,0:T(8,128)S(1)} fusion(f32[4,64,512]{2,1,0:T(8,128)S(1)} %convolution_bitcast_fusion, f32[4,64,512]{2,1,0:T(8,128)S(1)} %fusion.15, f32[64,512]{1,0:T(8,128)S(1)} %get-tuple-element.210, f32[64,512]{1,0:T(8,128)S(1)} %get-tuple-element.211), kind=kOutput, calls=%fused_computation.51 | convolution fusion | flops 809369600 | bytes 1835008 | tf_op jit(solution)/shard_map/ckq,qm->ckm/dot_general | solution.py:10
  44.1 5.4 %fusion.32 = f32[4,64,512]{2,1,0:T(8,128)S(1)} fusion(f32[4,64,512]{2,1,0:T(8,128)S(1)} %fusion.15, f32[4,64,512]{2,1,0:T(8,128)S(1)} %convolution_bitcast_fusion, f32[64,512]{1,0:T(8,128)S(1)} %get-tuple-element.210, f32[64,512]{1,0:T(8,128)S(1)} %get-tuple-element.211), kind=kOutput, calls=%fused_computation.53 | convolution fusion | flops 809369600 | bytes 1835008 | tf_op jit(solution)/shard_map/ckq,qm->ckm/dot_general | solution.py:10
  49.5 5.4 %convolution_subtract_fusion = f32[4,64,512]{2,1,0:T(8,128)S(1)} fusion(f32[4,64,512]{2,1,0:T(8,128)S(1)} %fusion.30, f32[4,64,512]{2,1,0:T(8,128)S(1)} %fusion.15, f32[4,64,512]{2,1,0:T(8,128)S(1)} %convolution_bitcast_fusion, f32[64,512]{1,0:T(8,128)S(1)} %get-tuple-element.210, f32[64,512]{1,0:T(8,128)S(1)} %get-tuple-element.211), kind=kOutput, calls=%fused_computation.28 | convolution fusion | flops 809500672 | bytes 2359296 | tf_op jit(solution)/shard_map/ckq,qm->ckm/dot_general | solution.py:10
  54.9 5.6 %convolution_add_fusion.1 = f32[4,64,512]{2,1,0:T(8,128)S(1)} fusion(f32[4,64,512]{2,1,0:T(8,128)S(1)} %fusion.32, f32[4,64,512]{2,1,0:T(8,128)S(1)} %convolution_bitcast_fusion, f32[4,64,512]{2,1,0:T(8,128)S(1)} %fusion.15, f32[64,512]{1,0:T(8,128)S(1)} %get-tuple-element.210, f32[64,512]{1,0:T(8,128)S(1)} %get-tuple-element.211), kind=kOutput, calls=%fused_computation.29 | convolution fusion | flops 809500672 | bytes 2359296 | tf_op jit(solution)/shard_map/ckq,qm->ckm/dot_general | solution.py:10
  60.6 4.9 %fusion.28 = f32[2,64,512]{2,1,0:T(8,128)S(1)} fusion(f32[2,64,512]{2,1,0:T(8,128)S(1)} %get-tuple-element.208), kind=kOutput, calls=%fused_computation.49 | convolution fusion | flops 406323200 | bytes 524288 | tf_op jit(solution)/shard_map/ckm,mq->ckq/dot_general | solution.py:10
  65.5 4.9 %fusion.26 = f32[2,64,512]{2,1,0:T(8,128)S(1)} fusion(f32[2,64,512]{2,1,0:T(8,128)S(1)} %get-tuple-element.209), kind=kOutput, calls=%fused_computation.47 | convolution fusion | flops 406323200 | bytes 524288 | tf_op jit(solution)/shard_map/ckm,mq->ckq/dot_general | solution.py:10
  70.4 4.9 %convolution_subtract_fusion.1 = f32[2,64,512]{2,1,0:T(8,128)S(1)} fusion(f32[2,64,512]{2,1,0:T(8,128)S(1)} %fusion.28, f32[2,64,512]{2,1,0:T(8,128)S(1)} %get-tuple-element.209), kind=kOutput, calls=%fused_computation.34 | convolution fusion | flops 406388736 | bytes 786432 | tf_op jit(solution)/shard_map/ckm,mq->ckq/dot_general | solution.py:10
  75.2 5.1 %convolution_add_fusion.2 = f32[2,64,512]{2,1,0:T(8,128)S(1)} fusion(f32[2,64,512]{2,1,0:T(8,128)S(1)} %fusion.26, f32[2,64,512]{2,1,0:T(8,128)S(1)} %get-tuple-element.208), kind=kOutput, calls=%fused_computation.33 | convolution fusion | flops 406388736 | bytes 786432 | tf_op jit(solution)/shard_map/ckm,mq->ckq/dot_general | solution.py:10
  82.2 3.9 %all-to-all-start.2 = ((bf16[32,2,512]{2,1,0:T(2,128)(2,1)}), bf16[32,2,512]{2,1,0:T(2,128)(2,1)S(1)}, u32[]{:S(2)}, u32[]{:S(2)}) async-start(bf16[32,2,512]{2,1,0:T(2,128)(2,1)} %reshape.134), calls=%async_computation.2 | async-start | bytes 131072 | tf_op jit(solution)/shard_map/all_to_all | solution.py:65
  86.5 7.1 %all-to-all-done.2 = bf16[32,2,512]{2,1,0:T(2,128)(2,1)S(1)} async-done(((bf16[32,2,512]{2,1,0:T(2,128)(2,1)}), bf16[32,2,512]{2,1,0:T(2,128)(2,1)S(1)}, u32[]{:S(2)}, u32[]{:S(2)}) %all-to-all-start.2) | async-done | bytes 65568 | tf_op jit(solution)/shard_map/all_to_all | solution.py:65
  94.1 28.8 %all_gather.10 = bf16[32,16,512]{0,1,2:T(8,128)(2,1)S(1)} all-gather(bf16[32,16,64]{0,1,2:T(8,128)(2,1)S(1)} %fusion.38), channel_id=1, replica_groups=mesh['seq'=32,'chan'=8] {'chan'}, dimensions={2}, use_global_device_ids=true | all-gather | bytes 589824 | tf_op jit(solution)/shard_map/all_gather | solution.py:88
  123.0 2.2 copy.86
  127.2 53.7 %all-gather.5.cloned.1.call-done = bf16[32,512,128]{2,1,0:T(8,128)(2,1)} async-done(((bf16[32,16,128]{2,1,0:T(8,128)(2,1)}), bf16[32,512,128]{2,1,0:T(8,128)(2,1)}) %all-gather.5.cloned.1.call-update) | async-done | bytes 4194320 | tf_op jit(solution)/shard_map/all_gather | solution.py:103
  180.8 56.5 %while.18 = (s32[]{:T(128)}, f32[512]{0:T(512)S(1)}, f32[512]{0:T(512)S(1)}, f32[512,128]{1,0:T(8,128)S(1)}, bf16[32,512,128]{2,1,0:T(8,128)(2,1)}, /*index=5*/b...) while((s32[]{:T(128)}, f32[512]{0:T(512)S(1)}, ...), condition=%wide.region_3.4_spmd.clone, body=%wide.region_0.3_spmd.clone.sunk | while | flops 277024832 | bytes 8589887 | solution.py:140
  184.7 1.1 constant_dynamic-slice_fusion.3
  191.7 1.1 constant_dynamic-slice_fusion.3
  202.3 1.1 constant_dynamic-slice_fusion.3
  209.4 1.1 constant_dynamic-slice_fusion.3
  220.0 1.1 constant_dynamic-slice_fusion.3
  (231 shorter events, 61.5 us)
Async XLA Ops:
  7.2 118.0 %copy-start = (bf16[512,128]{1,0:T(8,128)(2,1)S(1)}, bf16[512,128]{1,0:T(8,128)(2,1)}, u32[]{:S(2)}) copy-start(bf16[512,128]{1,0:T(8,128)(2,1)} %param.15) | copy-start | bytes 393220
  7.2 120.0 %all-gather.3.cloned.1.call-start = ((), (), s32[]{:S(2)}) async-start(), calls=%async_computation.3 | async-start | bytes 4325376 | tf_op jit(solution)/shard_map/all_gather | solution.py:102
  10.0 15.9 %all-to-all-start.1 = ((bf16[32,2,512]{2,1,0:T(2,128)(2,1)}), bf16[32,2,512]{2,1,0:T(2,128)(2,1)S(1)}, u32[]{:S(2)}, u32[]{:S(2)}) async-start(bf16[32,2,512]{2,1,0:T(2,128)(2,1)} %reshape.130), calls=%async_computation.1 | async-start | bytes 131072 | tf_op jit(solution)/shard_map/all_to_all | solution.py:18
  26.0 11.3 %all-to-all-start = ((bf16[32,2,512]{2,1,0:T(2,128)(2,1)}), bf16[32,2,512]{2,1,0:T(2,128)(2,1)S(1)}, u32[]{:S(2)}, u32[]{:S(2)}) async-start(bf16[32,2,512]{2,1,0:T(2,128)(2,1)} %reshape.132), calls=%async_computation | async-start | bytes 131072 | tf_op jit(solution)/shard_map/all_to_all | solution.py:15
  80.3 5.9 %copy-start.1 = (bf16[32,16,64]{2,1,0:T(8,128)(2,1)S(1)}, bf16[32,16,64]{2,1,0:T(8,128)(2,1)}, u32[]{:S(2)}) copy-start(bf16[32,16,64]{2,1,0:T(8,128)(2,1)} %param.10) | copy-start | bytes 196612
  81.2 12.8 %copy-start.2 = (f32[64]{0:T(128)S(1)}, f32[64]{0:T(128)}, u32[]{:S(2)}) copy-start(f32[64]{0:T(128)} %param.12) | copy-start | bytes 772
  82.2 11.4 %all-to-all-start.2 = ((bf16[32,2,512]{2,1,0:T(2,128)(2,1)}), bf16[32,2,512]{2,1,0:T(2,128)(2,1)S(1)}, u32[]{:S(2)}, u32[]{:S(2)}) async-start(bf16[32,2,512]{2,1,0:T(2,128)(2,1)} %reshape.134), calls=%async_computation.2 | async-start | bytes 131072 | tf_op jit(solution)/shard_map/all_to_all | solution.py:65
  86.2 94.6 %all-gather.5.cloned.1.call-start = ((), (), s32[]{:S(2)}) async-start(), calls=%async_computation.4 | async-start | bytes 4325376 | tf_op jit(solution)/shard_map/all_gather | solution.py:103
  123.0 57.8 %copy-start.3 = (bf16[32,16,128]{2,1,0:T(8,128)(2,1)S(1)}, bf16[32,16,128]{2,1,0:T(8,128)(2,1)}, u32[]{:S(2)}) copy-start(bf16[32,16,128]{2,1,0:T(8,128)(2,1)} %param.13) | copy-start | bytes 393220
Sparse Core Ops, SparseCore 0:
  10.5 58.7 all-gather.2
  126.3 54.5 all-gather.4
where the time goes:
time: 246 us; the launch traced here: 245 us
  waiting for transfers between devices  73.2 us (30%)
  matrix products  67.3 us (27%)
  blocking collectives  28.8 us (12%)
  local copies, waits for them, and re-layouts  28.4 us (12%)
  starting transfers between devices  16.5 us (7%)
  other arithmetic  15.3 us (6%)
  between operations  14.4 us (6%)
    all_gather x1, waiting for transfers between devices, body(): value_piece = lax.all_gather(values, 'seq', axis=1, tiled=True)  53.7 us
    dot_general x12, matrix products, mixdot(): return jnp.einsum(form, left, right, precision=lax.Precision.HIGHEST)  43.3 us
    all_gather x1, blocking collectives, body(): piece = lax.all_gather(conv_out, 'chan', axis=2, tiled=True)  28.8 us
    dynamic_slice x16, local copies, waits for them, and re-layouts, key_step(): lax.dynamic_slice_in_dim(value_piece, offset, step_size, 1)  17.2 us
    dot_general x16, matrix products, key_step(): jnp.dot(weights.astype(jnp.bfloat16), value_block, preferred_element_type...  15.7 us
    reduce_sum x16, other arithmetic, key_step(): row_total = row_total * factor + jnp.sum(weights, axis=1)  9.97 us
    all_to_all x1, starting transfers between devices, channel_convolve(): lax.all_to_all(long_filter.astype(jnp.bfloat16), 'seq', split_axis=2, con...  8.59 us
    dot_general x16, matrix products, key_step(): jnp.einsum('qd,kd->qk', query_rows, key_block, preferred_element_type=jnp...  7.38 us
  transfers between devices with their start and end apart: 5, of which 4 were waited for; matrix products, arithmetic and copies ran while one was open for 22% of the time, Pallas kernels for 0%

commit v1 on v0

v1 whole, which is shorter than its diff:
```python
import math

import jax
import jax.numpy as jnp
from jax import lax
from jax.experimental import pallas as pl
from jax.experimental.pallas import tpu as pltpu
from jax.sharding import PartitionSpec as P

MESH = pl.DeviceIdType.MESH
F32 = jnp.float32
BF16 = jnp.bfloat16
VM = pltpu.VMEM


def device_at(seq, chan):
    return (jnp.int32(seq), jnp.int32(chan))


def signal(target):
    pl.semaphore_signal(
        pltpu.get_barrier_semaphore(), inc=1, device_id=target, device_id_type=MESH
    )


def remote(src, dst, send, recv, target):
    return pltpu.make_async_remote_copy(
        src_ref=src,
        dst_ref=dst,
        send_sem=send,
        recv_sem=recv,
        device_id=target,
        device_id_type=MESH,
    )


def exchange_kernel(n, along_seq, spread, src, dst, send, recv, own):
    seq = lax.axis_index("seq")
    chan = lax.axis_index("chan")
    me = seq if along_seq else chan

    def peer(step):
        other = lax.rem(me + step, n)
        return other, (device_at(other, chan) if along_seq else device_at(seq, other))

    def greet(step, carry):
        signal(peer(step)[1])
        return carry

    lax.fori_loop(1, n, greet, 0)
    local = pltpu.make_async_copy(src if spread else src.at[me], dst.at[me], own)
    local.start()
    pl.semaphore_wait(pltpu.get_barrier_semaphore(), n - 1)

    def post(step, carry):
        other, target = peer(step)
        remote(
            src if spread else src.at[other], dst.at[me], send.at[step], recv.at[step], target
        ).start()
        return carry

    lax.fori_loop(1, n, post, 0)

    def finish(step, carry):
        other, target = peer(step)
        back = lax.rem(me + n - step, n)
        done = remote(
            src if spread else src.at[other], dst.at[back], send.at[step], recv.at[step], target
        )
        done.wait()
        return carry

    lax.fori_loop(1, n, finish, 0)
    local.wait()


def all_to_all(blocks, collective):
    n = blocks.shape[0]

    def kernel(src, dst, send, recv, own):
        exchange_kernel(n, True, False, src, dst, send, recv, own)

    return pl.pallas_call(
        kernel,
        out_shape=jax.ShapeDtypeStruct(blocks.shape, blocks.dtype),
        in_specs=[pl.BlockSpec(memory_space=VM)],
        out_specs=pl.BlockSpec(memory_space=VM),
        scratch_shapes=[
            pltpu.SemaphoreType.DMA((n,)),
            pltpu.SemaphoreType.DMA((n,)),
            pltpu.SemaphoreType.DMA,
        ],
        compiler_params=pltpu.CompilerParams(collective_id=collective, has_side_effects=True),
    )(blocks)


def project_values(mixed, w_value, n_chan):
    rows, tokens = mixed.shape

    def kernel(src, w_ref, out, held, send, recv, own):
        exchange_kernel(n_chan, False, True, src, held, send, recv, own)
        out[...] = lax.dot_general(
            held[...].reshape(n_chan * rows, tokens),
            w_ref[...],
            (((0,), (0,)), ((), ())),
            preferred_element_type=F32,
        ).astype(out.dtype)

    return pl.pallas_call(
        kernel,
        out_shape=jax.ShapeDtypeStruct((tokens, w_value.shape[1]), BF16),
        in_specs=[pl.BlockSpec(memory_space=VM)] * 2,
        out_specs=pl.BlockSpec(memory_space=VM),
        scratch_shapes=[
            pltpu.VMEM((n_chan, rows, tokens), BF16),
            pltpu.SemaphoreType.DMA((n_chan,)),
            pltpu.SemaphoreType.DMA((n_chan,)),
            pltpu.SemaphoreType.DMA,
        ],
        compiler_params=pltpu.CompilerParams(collective_id=2, has_side_effects=True),
    )(mixed, w_value)


SIDE = 4
COPIES = 26


class Gather:
    def __init__(self, own_ref, buf, send, recv, own_sem):
        seq = lax.axis_index("seq")
        self.chan = lax.axis_index("chan")
        self.own_ref, self.buf, self.send, self.recv, self.own_sem = (
            own_ref, buf, send, recv, own_sem
        )
        self.core = lax.rem(seq, 2)
        self.x = lax.rem(seq // 2, SIDE)
        self.y = seq // (2 * SIDE)
        self.half = own_ref.shape[0] // 2

    def at(self, y, x, core):
        return device_at((y * SIDE + x) * 2 + core, self.chan)

    def step(self, half, phase, by):
        along_x = (half == 0) == (phase == 1)
        if along_x:
            return self.at(self.y, lax.rem(self.x + by + SIDE, SIDE), self.core)
        return self.at(lax.rem(self.y + by + SIDE, SIDE), self.x, self.core)

    def block(self, half, phase, by):
        rows = pl.ds(half * self.half, self.half)
        along_x = (half == 0) == (phase == 1)
        y, x = self.y, self.x
        if along_x:
            x = lax.rem(x + by + SIDE, SIDE)
        else:
            y = lax.rem(y + by + SIDE, SIDE)
        return y, x, along_x, rows

    def one(self, half, by):
        y, x, _, rows = self.block(half, 1, by)
        return self.buf.at[y, x, self.core, rows]

    def row(self, half, by, core=None, part=None):
        y, x, along_x, rows = self.block(half, 2, by)
        core = self.core if core is None else core
        if part is not None:
            quarter = self.half // 2
            rows = pl.ds(half * self.half + part * quarter, quarter)
        if along_x:
            return self.buf.at[:, x, core, rows]
        return self.buf.at[y, :, core, rows]

    def sems(self, half, number):
        index = half * 13 + number
        return self.send.at[index], self.recv.at[index]

    def greet(self):
        for by in (1, 2, 3):
            signal(self.step(0, 1, by))
            signal(self.step(1, 1, by))
        signal(self.at(self.y, self.x, 1 - self.core))
        self.local = pltpu.make_async_copy(
            self.own_ref, self.buf.at[self.y, self.x, self.core], self.own_sem
        )
        self.local.start()
        pl.semaphore_wait(pltpu.get_barrier_semaphore(), 7)


    def first(self, half, i, landing=False):
        by = (1, -1, 2)[i]
        rows = pl.ds(half * self.half, self.half)
        dst = self.one(half, -by) if landing else self.one(half, 0)
        return remote(self.own_ref.at[rows], dst, *self.sems(half, i), self.step(half, 1, by))

    def second(self, half, i, landing=False):
        by = (1, -1)[i]
        dst = self.row(half, -by) if landing else self.row(half, 0)
        return remote(self.row(half, 0), dst, *self.sems(half, 3 + i), self.step(half, 2, by))

    def relay(self, half, i, landing=False):
        by = (1, -1)[i]
        src = self.row(half, -by, part=i)
        dst = self.row(half, 2, part=i) if landing else src
        return remote(src, dst, *self.sems(half, 5 + i), self.step(half, 2, by))

    def across(self, half, i, landing=False):
        by, part = ((0, None), (-1, None), (1, None), (2, 0), (2, 1))[i]
        src = self.row(half, by, part=part)
        dst = self.row(half, by, core=1 - self.core, part=part) if landing else src
        return remote(
            src, dst, *self.sems(half, 7 + i), self.at(self.y, self.x, 1 - self.core)
        )

    def start(self):
        self.greet()
        for i in range(3):
            for half in range(2):
                self.first(half, i).start()

    def middle(self):
        self.local.wait()
        for half in range(2):
            for i in range(3):
                self.first(half, i, True).wait_recv()
            for i in range(2):
                self.second(half, i).start()
        for half in range(2):
            self.across(half, 0).start()

    def late(self):
        for i in range(2):
            for half in range(2):
                self.second(half, i, True).wait_recv()
                self.relay(half, i).start()
        for i in range(2):
            for half in range(2):
                self.across(half, 1 + i).start()

    def last(self):
        for i in range(2):
            for half in range(2):
                self.relay(half, i, True).wait_recv()
                self.across(half, 3 + i).start()

    def end(self):
        for half in range(2):
            for i in range(5):
                self.across(half, i, True).wait_recv()
        for half in range(2):
            for i in range(3):
                self.first(half, i).wait_send()
            for i in range(2):
                self.second(half, i).wait_send()
                self.relay(half, i).wait_send()
            for i in range(5):
                self.across(half, i).wait_send()


def gather_scratch():
    return [
        pltpu.SemaphoreType.DMA((COPIES,)),
        pltpu.SemaphoreType.DMA((COPIES,)),
        pltpu.SemaphoreType.DMA,
    ]


TILE = 128
GROUP = 16


def spread_taps(h_ref, base, ch):
    wide = jnp.broadcast_to(h_ref[ch], (8, h_ref.shape[2])).astype(F32)
    sub = lax.broadcasted_iota(jnp.int32, wide.shape, 0)
    for bit in (1, 2, 4):
        wide = jnp.where((sub & bit) != 0, pltpu.roll(wide, bit, 1), wide)
    base[...] = wide


def spread_signal(x_ref, shifted, ch):
    x = x_ref[ch].astype(F32)
    row = lax.broadcasted_iota(jnp.int32, x.shape, 0)
    for k in range(GROUP):
        moved = x if k == 0 else jnp.where(row >= k, pltpu.roll(x, k, 0), 0.0)
        lanes = pl.ds((k % 2) * TILE, TILE)
        shifted[k // 2, :, lanes] = moved.astype(BF16)


def toeplitz(base, lane):
    parts = []
    for half in range(2):
        window = base[:, pl.ds(pl.multiple_of(lane + half * TILE, TILE), 2 * TILE)]
        for u in range(TILE // 8):
            moved = window if u == 0 else pltpu.roll(window, 8 * u, 1)
            parts.append(moved[:, TILE:])
    return jnp.concatenate(parts, axis=0).astype(BF16)


def convolve_channel(x_ref, h_ref, y_ref, base, shifted, total, ch):
    blocks = x_ref.shape[1]
    spread_taps(h_ref, base, ch)
    spread_signal(x_ref, shifted, ch)
    for g in range(blocks // GROUP):
        rows = blocks - GROUP * g

        def pair(kk, acc, g=g, rows=rows):
            block = toeplitz(base, (GROUP * g + 2 * kk) * TILE)
            left = shifted[kk, pl.ds(0, rows), :]
            return acc + jnp.dot(left, block, preferred_element_type=F32)

        acc = lax.fori_loop(0, GROUP // 2, pair, jnp.zeros((rows, TILE), F32), unroll=2)
        if g == 0:
            total[...] = acc
        else:
            total[pl.ds(GROUP * g, rows), :] += acc
    y_ref[ch] = total[...].astype(BF16)


def conv_and_keys(x, h, keys):
    tokens, head = keys.shape

    def kernel(x_ref, h_ref, k_ref, y_ref, buf, base, shifted, total, send, recv, own):
        gather = Gather(k_ref, buf, send, recv, own)
        gather.start()
        spare = x_ref.shape[0]
        convolve_channel(x_ref, h_ref, y_ref, base, shifted, total, 0)
        gather.middle()
        for ch in range(1, spare):
            convolve_channel(x_ref, h_ref, y_ref, base, shifted, total, ch)
        gather.late()
        gather.last()
        gather.end()

    blocks = x.shape[1]
    return pl.pallas_call(
        kernel,
        out_shape=(
            jax.ShapeDtypeStruct(x.shape, BF16),
            jax.ShapeDtypeStruct((SIDE, SIDE, 2, tokens, head), BF16),
        ),
        in_specs=[pl.BlockSpec(memory_space=VM)] * 3,
        out_specs=(pl.BlockSpec(memory_space=VM),) * 2,
        scratch_shapes=[
            pltpu.VMEM((8, h.shape[2]), F32),
            pltpu.VMEM((GROUP // 2, blocks, 2 * TILE), BF16),
            pltpu.VMEM((blocks, TILE), F32),
        ]
        + gather_scratch(),
        compiler_params=pltpu.CompilerParams(collective_id=1, has_side_effects=True),
    )(x, h, keys)


QROWS = 128


def key_block(buf, index, slab):
    part = buf[:, :, :, pl.ds(pl.multiple_of(index * slab, slab), slab), :]
    return part.reshape(2 * SIDE * SIDE * slab, part.shape[-1])


def fold(values, combine):
    out = values[:, :TILE]
    for start in range(TILE, values.shape[1], TILE):
        out = combine(out, values[:, start : start + TILE])
    return out


def attend(queries, keys, values, slab):
    tokens, head = queries.shape
    scale = math.log2(math.e) / math.sqrt(head)
    width = 2 * SIDE * SIDE * slab
    per_tile = QROWS // slab
    tiles = tokens // QROWS

    def kernel(q_ref, k_buf, v_ref, out, buf, weights, totals, send, recv, own):
        first_row = lax.axis_index("seq") * slab
        row = lax.broadcasted_iota(jnp.int32, (QROWS, width), 0)
        lane = lax.broadcasted_iota(jnp.int32, (QROWS, width), 1)

        def scores(q, block):
            return lax.dot_general(
                q, key_block(k_buf, block, slab), (((1,), (1,)), ((), ())),
                preferred_element_type=F32,
            )

        def allowed(tile, block):
            return (block - tile * per_tile) * width + lane <= (
                (row // slab) * width + first_row + row % slab
            )

        def weigh(tile):
            q = q_ref[pl.ds(tile * QROWS, QROWS), :]
            whole = tile * per_tile

            def best_whole(block, best):
                return jnp.maximum(best, fold(scores(q, block), jnp.maximum))

            def best_edge(block, best):
                s = jnp.where(allowed(tile, block), scores(q, block), -1e30)
                return jnp.maximum(best, fold(s, jnp.maximum))

            best = jnp.full((QROWS, TILE), -1e30, F32)
            best = lax.fori_loop(0, whole, best_whole, best)
            best = lax.fori_loop(whole, whole + per_tile, best_edge, best)
            best = jnp.max(best, axis=1, keepdims=True)

            def put(block, w):
                lanes = pl.ds(pl.multiple_of(block * width, width), width)
                weights[pl.ds(tile * QROWS, QROWS), lanes] = w.astype(BF16)

            def weigh_whole(block, total):
                w = jnp.exp2((scores(q, block) - best) * scale)
                put(block, w)
                return total + fold(w, jnp.add)

            def weigh_edge(block, total):
                w = jnp.exp2((scores(q, block) - best) * scale)
                w = jnp.where(allowed(tile, block), w, 0.0)
                put(block, w)
                return total + fold(w, jnp.add)

            total = jnp.zeros((QROWS, TILE), F32)
            total = lax.fori_loop(0, whole, weigh_whole, total)
            total = lax.fori_loop(whole, whole + per_tile, weigh_edge, total)
            totals[pl.ds(tile * QROWS, QROWS), :] = jnp.broadcast_to(
                jnp.sum(total, axis=1, keepdims=True), (QROWS, TILE)
            )

        gather = Gather(v_ref, buf, send, recv, own)
        gather.start()
        weigh(0)
        gather.middle()
        weigh(1)
        weigh(2)
        gather.late()
        weigh(3)
        gather.last()
        gather.end()

        for tile in range(tiles):
            rows = pl.ds(tile * QROWS, QROWS)

            def add(block, acc, rows=rows):
                lanes = pl.ds(pl.multiple_of(block * width, width), width)
                return acc + jnp.dot(
                    weights[rows, lanes], key_block(buf, block, slab), preferred_element_type=F32
                )

            acc = lax.fori_loop(
                0, (tile + 1) * per_tile, add, jnp.zeros((QROWS, head), F32), unroll=4
            )
            out[rows, :] = (acc / totals[rows, :]).astype(BF16)

    return pl.pallas_call(
        kernel,
        out_shape=jax.ShapeDtypeStruct((tokens, head), BF16),
        in_specs=[pl.BlockSpec(memory_space=VM)] * 3,
        out_specs=pl.BlockSpec(memory_space=VM),
        scratch_shapes=[
            pltpu.VMEM((SIDE, SIDE, 2, tokens, head), BF16),
            pltpu.VMEM((tokens, tokens * 2 * SIDE * SIDE), BF16),
            pltpu.VMEM((tokens, TILE), F32),
        ]
        + gather_scratch(),
        compiler_params=pltpu.CompilerParams(collective_id=3, has_side_effects=True),
    )(queries, keys, values)


def body(n_chan, conv_in, conv_gate, long_filter, skip_gain, queries, keys_in, w_value):
    blocks, slab, channels = conv_in.shape
    tokens = blocks * slab
    n_seq = 2 * SIDE * SIDE
    each = channels // n_seq
    length = tokens * n_seq
    lines = tokens // TILE
    signal_t = conv_in.reshape(tokens, channels).T
    taps_t = long_filter.reshape(tokens, channels).astype(BF16).T
    packed = jnp.stack(
        [signal_t.reshape(n_seq, each, tokens), taps_t.reshape(n_seq, each, tokens)], axis=1
    ).reshape(n_seq, 2 * each * lines, TILE)
    got = all_to_all(packed, 0)
    whole = (
        got.reshape(n_seq, 2, each, blocks, slab).transpose(1, 2, 3, 0, 4).reshape(2, each, length)
    )
    x = whole[0].reshape(each, length // TILE, TILE)
    h = jnp.pad(whole[1].astype(F32), ((0, 0), (TILE, 0))).reshape(each, 1, length + TILE)
    y, keys = conv_and_keys(x, h, keys_in.reshape(tokens, -1))
    back = (
        y.reshape(each, blocks, n_seq, slab)
        .transpose(2, 0, 1, 3)
        .reshape(n_seq, each * lines, TILE)
    )
    convolved = all_to_all(back, 4).reshape(channels, tokens).astype(F32)
    gate_t = conv_gate.reshape(tokens, channels).T
    mixed_t = (
        (convolved + skip_gain[:, None] * signal_t.astype(F32)) * gate_t.astype(F32)
    ).astype(BF16)
    conv_out = mixed_t.T.reshape(blocks, slab, channels)
    values = project_values(mixed_t, w_value, n_chan)
    attended = attend(queries.reshape(tokens, -1), keys, values, slab)
    return conv_out, attended.reshape(blocks, slab, -1)


def solution(mesh):
    n_chan = mesh.shape["chan"]

    def local(*args):
        return body(n_chan, *args)

    spec = P(None, "seq", "chan")
    return jax.shard_map(
        local,
        mesh=mesh,
        in_specs=(spec, spec, spec, P("chan"), spec, spec, P(None, "chan")),
        out_specs=(spec, spec),
        check_vma=False,
    )
```

time: 246 us -> 140 us (0.57)
  Pallas kernels: 0 us -> 125 us
  waiting for transfers between devices: 73.2 us -> 0 us
  matrix products: 67.3 us -> 0 us
  blocking collectives: 28.8 us -> 0 us
  local copies, waits for them, and re-layouts: 28.4 us -> 11.6 us
  starting transfers between devices: 16.5 us -> 0 us
  between operations: 14.4 us -> 0.81 us
  other arithmetic: 15.3 us -> 1.96 us
    pallas_call x0 -> x5, Pallas kernels: none -> 125 us  [the longest x1 48.4 us: attend(): pl.pallas_call(kernel, out_shape=jax.ShapeDtypeStruct((tokens, head), BF1...]
    dot_general x45 -> x0, matrix products: 67.3 us -> none  [the longest x12 43.3 us: mixdot(): return jnp.einsum(form, left, right, precision=lax.Precision.HIGHEST)]
    all_gather x2 -> x0, waiting for transfers between devices: 53.7 us -> none  [the longest x1 53.7 us: body(): value_piece = lax.all_gather(values, 'seq', axis=1, tiled=True)]
    all_gather x1 -> x0, blocking collectives: 28.8 us -> none  [body(): piece = lax.all_gather(conv_out, 'chan', axis=2, tiled=True)]
    all_to_all x3 -> x0, waiting for transfers between devices: 18.9 us -> none  [the longest x1 7.08 us: channel_convolve(): lax.all_to_all(result.transpose(1, 2, 0).astype(jnp.bfloat16), 'seq', spl...]
    dynamic_slice x16 -> x0, local copies, waits for them, and re-layouts: 17.2 us -> none  [key_step(): lax.dynamic_slice_in_dim(value_piece, offset, step_size, 1)]
    all_to_all x3 -> x0, starting transfers between devices: 16.4 us -> none  [the longest x1 8.59 us: channel_convolve(): lax.all_to_all(long_filter.astype(jnp.bfloat16), 'seq', split_axis=2, con...]
    reduce_sum x16 -> x0, other arithmetic: 9.97 us -> none  [key_step(): row_total = row_total * factor + jnp.sum(weights, axis=1)]
  transfers between devices with their start and end apart: 5 -> 0, of which waited for: 4 -> 0; matrix products, arithmetic and copies ran while one was open for 22% -> 0% of each run, Pallas kernels for 0% -> 0%
where the time goes in v1:
time: 140 us; the launch traced here: 139 us
  Pallas kernels  125 us (89%)
  local copies, waits for them, and re-layouts  11.6 us (8%)
  other arithmetic  1.96 us (1%)
    pallas_call x1, Pallas kernels, attend(): pl.pallas_call(kernel, out_shape=jax.ShapeDtypeStruct((tokens, head), BF1...  48.4 us
    pallas_call x1, Pallas kernels, conv_and_keys(): pl.pallas_call(kernel, out_shape=(jax.ShapeDtypeStruct(x.shape, BF16), ja...  32.1 us
    pallas_call x2, Pallas kernels, all_to_all(): pl.pallas_call(kernel, out_shape=jax.ShapeDtypeStruct(blocks.shape, block...  22.6 us
    pallas_call x1, Pallas kernels, project_values(): pl.pallas_call(kernel, out_shape=jax.ShapeDtypeStruct((tokens, w_value.sh...  21.8 us

profile of v1, /device:TPU:1, one launch (start us, length us, event | category | flops | bytes accessed | tf_op | source)
XLA Modules:
  0.0 139.2 jit_solution(6732894094148341389)
XLA Ops:
  0.6 1.0 copy.16
  1.7 1.0 convert_element_type.33
  2.6 0.1 copy.17
  2.8 0.2 pad_maximum_fusion
  3.1 0.7 reshape.53.src
  3.8 13.1 %shard_map.86 = bf16[32,16,128]{2,1,0:T(8,128)(2,1)} custom-call(bf16[32,16,128]{2,1,0:T(8,128)(2,1)} %reshape.53.src), custom_call_target="tpu_custom_call" | custom-call | tf_op jit(solution)/shard_map/pallas_call | solution.py:83
  16.9 1.2 copy.19
  18.2 0.3 copy.21
  18.4 0.5 convert_element_type.35
  19.1 0.7 reshape.64.h_ref
  19.8 0.3 copy.20
  20.1 1.0 reshape_squeeze.3.x_ref
  21.0 32.1 %shard_map.87 = (bf16[2,128,128]{2,1,0:T(8,128)(2,1)}, bf16[4,4,2,512,128]{4,3,2,1,0:T(8,128)(2,1)}) custom-call(bf16[2,128,128]{2,1,0:T(8,128)(2,1)} %reshape_squeeze.3.x_ref, f32[2,1,16512]{2,1,0:T(1,128)} %reshape.64.h_ref, bf16[512,128]{1,0:T(8,128)(2,1)} %bitcast.37), custom_call_target="tpu_custom_call" | custom-call | tf_op jit(solution)/shard_map/pallas_call | solution.py:334
  53.1 1.2 reshape.58
  54.3 0.2 copy.22
  54.5 0.8 copy.23.src
  55.3 9.5 %shard_map.88 = bf16[32,8,128]{2,1,0:T(8,128)(2,1)} custom-call(bf16[32,8,128]{2,1,0:T(8,128)(2,1)} %copy.23.src), custom_call_target="tpu_custom_call" | custom-call | tf_op jit(solution)/shard_map/pallas_call | solution.py:83
  64.9 0.9 reshape.65
  65.8 0.1 copy.24
  65.9 0.7 fusion.src
  66.6 21.8 %shard_map.89.v_ref = bf16[512,128]{1,0:T(8,128)(2,1)} custom-call(bf16[64,512]{1,0:T(8,128)(2,1)} %fusion.src, bf16[512,128]{1,0:T(8,128)(2,1)} %w_ref.1), custom_call_target="tpu_custom_call" | custom-call | tf_op jit(solution)/shard_map/pallas_call | solution.py:109
  88.4 48.4 %shard_map.90 = bf16[512,128]{1,0:T(8,128)(2,1)} custom-call(bf16[512,128]{1,0:T(8,128)(2,1)} %bitcast.34, bf16[4,4,2,512,128]{4,3,2,1,0:T(8,128)(2,1)} %get-tuple-element.5.k_buf, bf16[512,128]{1,0:T(8,128)(2,1)} %shard_map.89.v_ref), custom_call_target="tpu_custom_call" | custom-call | tf_op jit(solution)/shard_map/pallas_call | solution.py:453
  136.9 0.8 copy.25
  137.6 1.6 %copy.27 = bf16[32,16,128]{2,1,0:T(8,128)(2,1)} copy(bf16[32,16,128]{2,1,0:T(8,128)(2,1)} %bitcast.32) | data formatting | bytes 262144
  (12 shorter events, 0.3 us)
Async XLA Ops:
  2.8 63.0 %copy-start.1 = (bf16[32,16,64]{2,1,0:T(8,128)(2,1)S(1)}, bf16[32,16,64]{2,1,0:T(8,128)(2,1)}, u32[]{:S(2)}) copy-start(bf16[32,16,64]{2,1,0:T(8,128)(2,1)} %param.8) | copy-start | bytes 196612
  3.8 62.1 %copy-start.2 = (f32[64]{0:T(128)S(1)}, f32[64]{0:T(128)}, u32[]{:S(2)}) copy-start(f32[64]{0:T(128)} %param.10) | copy-start | bytes 772
  66.6 70.2 %copy-start = (bf16[64,512]{1,0:T(8,128)(2,1)S(1)}, bf16[64,512]{1,0:T(8,128)(2,1)}, u32[]{:S(2)}) copy-start(bf16[64,512]{1,0:T(8,128)(2,1)} %fusion.src) | copy-start | bytes 196612

commit v2 on v1

--- a/solution.py
+++ b/solution.py
@@ -94,33 +94,6 @@
     )(blocks)
 
 
-def project_values(mixed, w_value, n_chan):
-    rows, tokens = mixed.shape
-
-    def kernel(src, w_ref, out, held, send, recv, own):
-        exchange_kernel(n_chan, False, True, src, held, send, recv, own)
-        out[...] = lax.dot_general(
-            held[...].reshape(n_chan * rows, tokens),
-            w_ref[...],
-            (((0,), (0,)), ((), ())),
-            preferred_element_type=F32,
-        ).astype(out.dtype)
-
-    return pl.pallas_call(
-        kernel,
-        out_shape=jax.ShapeDtypeStruct((tokens, w_value.shape[1]), BF16),
-        in_specs=[pl.BlockSpec(memory_space=VM)] * 2,
-        out_specs=pl.BlockSpec(memory_space=VM),
-        scratch_shapes=[
-            pltpu.VMEM((n_chan, rows, tokens), BF16),
-            pltpu.SemaphoreType.DMA((n_chan,)),
-            pltpu.SemaphoreType.DMA((n_chan,)),
-            pltpu.SemaphoreType.DMA,
-        ],
-        compiler_params=pltpu.CompilerParams(collective_id=2, has_side_effects=True),
-    )(mixed, w_value)
-
-
 SIDE = 4
 COPIES = 26
 
@@ -179,11 +152,7 @@
             signal(self.step(0, 1, by))
             signal(self.step(1, 1, by))
         signal(self.at(self.y, self.x, 1 - self.core))
-        self.local = pltpu.make_async_copy(
-            self.own_ref, self.buf.at[self.y, self.x, self.core], self.own_sem
-        )
-        self.local.start()
-        pl.semaphore_wait(pltpu.get_barrier_semaphore(), 7)
+        return 7
 
 
     def first(self, half, i, landing=False):
@@ -212,7 +181,10 @@
         )
 
     def start(self):
-        self.greet()
+        self.local = pltpu.make_async_copy(
+            self.own_ref, self.buf.at[self.y, self.x, self.core], self.own_sem
+        )
+        self.local.start()
         for i in range(3):
             for half in range(2):
                 self.first(half, i).start()
@@ -281,38 +253,35 @@
     row = lax.broadcasted_iota(jnp.int32, x.shape, 0)
     for k in range(GROUP):
         moved = x if k == 0 else jnp.where(row >= k, pltpu.roll(x, k, 0), 0.0)
-        lanes = pl.ds((k % 2) * TILE, TILE)
-        shifted[k // 2, :, lanes] = moved.astype(BF16)
+        lanes = pl.ds((k % AT_ONCE) * TILE, TILE)
+        shifted[k // AT_ONCE, :, lanes] = moved.astype(BF16)
+
+
+AT_ONCE = 4
 
 
 def toeplitz(base, lane):
+    window = base[:, pl.ds(pl.multiple_of(lane, TILE), (AT_ONCE + 1) * TILE)]
+    moved = [window if u == 0 else pltpu.roll(window, 8 * u, 1) for u in range(TILE // 8)]
     parts = []
-    for half in range(2):
-        window = base[:, pl.ds(pl.multiple_of(lane + half * TILE, TILE), 2 * TILE)]
-        for u in range(TILE // 8):
-            moved = window if u == 0 else pltpu.roll(window, 8 * u, 1)
-            parts.append(moved[:, TILE:])
+    for d in range(AT_ONCE):
+        parts += [m[:, (d + 1) * TILE : (d + 2) * TILE] for m in moved]
     return jnp.concatenate(parts, axis=0).astype(BF16)
 
 
-def convolve_channel(x_ref, h_ref, y_ref, base, shifted, total, ch):
-    blocks = x_ref.shape[1]
-    spread_taps(h_ref, base, ch)
-    spread_signal(x_ref, shifted, ch)
-    for g in range(blocks // GROUP):
-        rows = blocks - GROUP * g
-
-        def pair(kk, acc, g=g, rows=rows):
-            block = toeplitz(base, (GROUP * g + 2 * kk) * TILE)
-            left = shifted[kk, pl.ds(0, rows), :]
-            return acc + jnp.dot(left, block, preferred_element_type=F32)
-
-        acc = lax.fori_loop(0, GROUP // 2, pair, jnp.zeros((rows, TILE), F32), unroll=2)
-        if g == 0:
-            total[...] = acc
-        else:
-            total[pl.ds(GROUP * g, rows), :] += acc
-    y_ref[ch] = total[...].astype(BF16)
+def convolve_group(base, shifted, total, g, blocks):
+    rows = blocks - GROUP * g
+
+    def some(kk, acc):
+        block = toeplitz(base, (GROUP * g + AT_ONCE * kk) * TILE)
+        left = shifted[kk, pl.ds(0, rows), :]
+        return acc + jnp.dot(left, block, preferred_element_type=F32)
+
+    acc = lax.fori_loop(0, GROUP // AT_ONCE, some, jnp.zeros((rows, TILE), F32), unroll=2)
+    if g == 0:
+        total[...] = acc
+    else:
+        total[pl.ds(GROUP * g, rows), :] += acc
 
 
 def conv_and_keys(x, h, keys):
@@ -320,14 +289,17 @@
 
     def kernel(x_ref, h_ref, k_ref, y_ref, buf, base, shifted, total, send, recv, own):
         gather = Gather(k_ref, buf, send, recv, own)
+        pl.semaphore_wait(pltpu.get_barrier_semaphore(), gather.greet())
         gather.start()
-        spare = x_ref.shape[0]
-        convolve_channel(x_ref, h_ref, y_ref, base, shifted, total, 0)
-        gather.middle()
-        for ch in range(1, spare):
-            convolve_channel(x_ref, h_ref, y_ref, base, shifted, total, ch)
-        gather.late()
-        gather.last()
+        stages = {(0, 1): gather.middle, (0, 7): gather.late, (1, 1): gather.last}
+        for ch in range(x_ref.shape[0]):
+            spread_taps(h_ref, base, ch)
+            spread_signal(x_ref, shifted, ch)
+            for g in range(x_ref.shape[1] // GROUP):
+                convolve_group(base, shifted, total, g, x_ref.shape[1])
+                if (ch, g) in stages:
+                    stages[ch, g]()
+            y_ref[ch] = total[...].astype(BF16)
         gather.end()
 
     blocks = x.shape[1]
@@ -341,7 +313,7 @@
         out_specs=(pl.BlockSpec(memory_space=VM),) * 2,
         scratch_shapes=[
             pltpu.VMEM((8, h.shape[2]), F32),
-            pltpu.VMEM((GROUP // 2, blocks, 2 * TILE), BF16),
+            pltpu.VMEM((GROUP // AT_ONCE, blocks, AT_ONCE * TILE), BF16),
             pltpu.VMEM((blocks, TILE), F32),
         ]
         + gather_scratch(),
@@ -357,112 +329,189 @@
     return part.reshape(2 * SIDE * SIDE * slab, part.shape[-1])
 
 
-def fold(values, combine):
-    out = values[:, :TILE]
-    for start in range(TILE, values.shape[1], TILE):
-        out = combine(out, values[:, start : start + TILE])
-    return out
-
-
-def attend(queries, keys, values, slab):
+class Ring:
+    def __init__(self, n, src, held, send, recv, own):
+        self.n, self.src, self.held, self.send, self.recv, self.own = n, src, held, send, recv, own
+        self.seq = lax.axis_index("seq")
+        self.me = lax.axis_index("chan")
+        self.steps = n // 2
+
+    def greet(self):
+        signal(device_at(self.seq, lax.rem(self.me + 1, self.n)))
+        signal(device_at(self.seq, lax.rem(self.me + self.n - 1, self.n)))
+        return 2
+
+    def copy(self, k, side, landing=False):
+        way = (1, -1)[side]
+        away = k if landing else k - 1
+        block = lax.rem(self.me - way * away + self.n, self.n)
+        half = self.src.shape[0] // 2
+        rows = pl.ds(side * half, half) if k == self.steps else pl.ds(0, 2 * half)
+        dst = self.held.at[block, rows]
+        src = self.src.at[rows] if k == 1 else dst
+        index = 2 * (k - 1) + side
+        target = device_at(self.seq, lax.rem(self.me + way + self.n, self.n))
+        return remote(src, dst, self.send.at[index], self.recv.at[index], target)
+
+    def start(self, k):
+        if k == 1:
+            self.local = pltpu.make_async_copy(self.src, self.held.at[self.me], self.own)
+            self.local.start()
+        for side in range(2):
+            if k > 1:
+                self.copy(k - 1, side, True).wait_recv()
+            self.copy(k, side).start()
+
+    def end(self):
+        for side in range(2):
+            self.copy(self.steps, side, True).wait_recv()
+        self.local.wait()
+        for k in range(1, self.steps + 1):
+            for side in range(2):
+                self.copy(k, side).wait_send()
+
+
+def attend(queries, keys, mixed, w_value, slab, n_chan):
     tokens, head = queries.shape
     scale = math.log2(math.e) / math.sqrt(head)
     width = 2 * SIDE * SIDE * slab
     per_tile = QROWS // slab
-    tiles = tokens // QROWS
-
-    def kernel(q_ref, k_buf, v_ref, out, buf, weights, totals, send, recv, own):
+    groups = width // TILE
+    pv_blocks = 2
+
+    def kernel(
+        q_ref, k_buf, m_ref, w_ref, out, buf, weights, best, totals, acc, held, value,
+        send, recv, own, ring_send, ring_recv, ring_own,
+    ):
         first_row = lax.axis_index("seq") * slab
-        row = lax.broadcasted_iota(jnp.int32, (QROWS, width), 0)
-        lane = lax.broadcasted_iota(jnp.int32, (QROWS, width), 1)
-
-        def scores(q, block):
+        row = lax.broadcasted_iota(jnp.int32, (QROWS, TILE), 0)
+        lane = lax.broadcasted_iota(jnp.int32, (QROWS, TILE), 1)
+        limit = (row // slab) * width + first_row + row % slab - lane
+
+        def scores(tile, block):
+            q = q_ref[pl.ds(tile * QROWS, tokens - tile * QROWS), :]
             return lax.dot_general(
                 q, key_block(k_buf, block, slab), (((1,), (1,)), ((), ())),
                 preferred_element_type=F32,
             )
 
-        def allowed(tile, block):
-            return (block - tile * per_tile) * width + lane <= (
-                (row // slab) * width + first_row + row % slab
-            )
-
-        def weigh(tile):
-            q = q_ref[pl.ds(tile * QROWS, QROWS), :]
-            whole = tile * per_tile
-
-            def best_whole(block, best):
-                return jnp.maximum(best, fold(scores(q, block), jnp.maximum))
-
-            def best_edge(block, best):
-                s = jnp.where(allowed(tile, block), scores(q, block), -1e30)
-                return jnp.maximum(best, fold(s, jnp.maximum))
-
-            best = jnp.full((QROWS, TILE), -1e30, F32)
-            best = lax.fori_loop(0, whole, best_whole, best)
-            best = lax.fori_loop(whole, whole + per_tile, best_edge, best)
-            best = jnp.max(best, axis=1, keepdims=True)
-
-            def put(block, w):
-                lanes = pl.ds(pl.multiple_of(block * width, width), width)
-                weights[pl.ds(tile * QROWS, QROWS), lanes] = w.astype(BF16)
-
-            def weigh_whole(block, total):
-                w = jnp.exp2((scores(q, block) - best) * scale)
-                put(block, w)
-                return total + fold(w, jnp.add)
-
-            def weigh_edge(block, total):
-                w = jnp.exp2((scores(q, block) - best) * scale)
-                w = jnp.where(allowed(tile, block), w, 0.0)
-                put(block, w)
-                return total + fold(w, jnp.add)
-
-            total = jnp.zeros((QROWS, TILE), F32)
-            total = lax.fori_loop(0, whole, weigh_whole, total)
-            total = lax.fori_loop(whole, whole + per_tile, weigh_edge, total)
-            totals[pl.ds(tile * QROWS, QROWS), :] = jnp.broadcast_to(
-                jnp.sum(total, axis=1, keepdims=True), (QROWS, TILE)
-            )
-
-        gather = Gather(v_ref, buf, send, recv, own)
+        def allowed(tile, block, part):
+            return (block - tile * per_tile) * width + part * TILE <= limit
+
+        def edge(tile, block, part, values, other):
+            top = jnp.where(allowed(tile, block, part), values[:QROWS], other)
+            if values.shape[0] == QROWS:
+                return top
+            return jnp.concatenate([top, values[QROWS:]], axis=0)
+
+        def find_best(tile, low, high):
+            rows = pl.ds(tile * QROWS, tokens - tile * QROWS)
+
+            def one(block, carry):
+                s = scores(tile, block)
+                top = best[rows, :]
+                for part in range(groups):
+                    piece = s[:, part * TILE : (part + 1) * TILE]
+                    top = jnp.maximum(top, edge(tile, block, part, piece, -1e30))
+                best[rows, :] = top
+                return carry
+
+            lax.fori_loop(tile * per_tile + low, tile * per_tile + high, one, 0)
+
+        def weigh(tile, low, high):
+            rows = pl.ds(tile * QROWS, tokens - tile * QROWS)
+
+            def one(block, carry):
+                s = scores(tile, block)
+                top = best[rows, :]
+                total = totals[rows, :]
+                for part in range(groups):
+                    piece = s[:, part * TILE : (part + 1) * TILE]
+                    w = jnp.exp2((piece - top) * scale)
+                    w = edge(tile, block, part, w, 0.0)
+                    lanes = pl.ds(pl.multiple_of(block * width + part * TILE, TILE), TILE)
+                    weights[rows, lanes] = w.astype(BF16)
+                    total = total + w
+                totals[rows, :] = total
+                return carry
+
+            lax.fori_loop(tile * per_tile + low, tile * per_tile + high, one, 0)
+
+        ring = Ring(n_chan, m_ref, held, ring_send, ring_recv, ring_own)
+        gather = Gather(value, buf, send, recv, own)
+        greeted = ring.greet() + gather.greet()
+        pl.semaphore_wait(pltpu.get_barrier_semaphore(), greeted)
+
+        ring.start(1)
+        best[...] = jnp.full(best.shape, -1e30, F32)
+        totals[...] = jnp.zeros(totals.shape, F32)
+        find_best(0, 0, 4)
+        ring.start(2)
+        find_best(0, 4, 8)
+        ring.start(3)
+        find_best(1, 0, 8)
+        ring.start(4)
+        find_best(2, 0, 8)
+        find_best(3, 0, 8)
+        best[...] = jnp.broadcast_to(jnp.max(best[...], axis=1, keepdims=True), best.shape)
+        ring.end()
+        value[...] = lax.dot_general(
+            held[...].reshape(held.shape[0] * held.shape[1], tokens),
+            w_ref[...],
+            (((0,), (0,)), ((), ())),
+            preferred_element_type=F32,
+        ).astype(BF16)
+        weigh(3, 0, 8)
         gather.start()
-        weigh(0)
+        weigh(2, 0, 8)
+        weigh(1, 0, 4)
         gather.middle()
-        weigh(1)
-        weigh(2)
+        weigh(1, 4, 8)
+        weigh(0, 0, 4)
         gather.late()
-        weigh(3)
+        weigh(0, 4, 8)
         gather.last()
         gather.end()
 
-        for tile in range(tiles):
-            rows = pl.ds(tile * QROWS, QROWS)
-
-            def add(block, acc, rows=rows):
-                lanes = pl.ds(pl.multiple_of(block * width, width), width)
-                return acc + jnp.dot(
-                    weights[rows, lanes], key_block(buf, block, slab), preferred_element_type=F32
+        acc[...] = jnp.zeros(acc.shape, F32)
+        for tile in range(tokens // QROWS):
+            rows = pl.ds(tile * QROWS, tokens - tile * QROWS)
+
+            def add(step, carry, rows=rows, tile=tile):
+                block = tile * per_tile + step * pv_blocks
+                lanes = pl.ds(pl.multiple_of(block * width, width), pv_blocks * width)
+                right = jnp.concatenate(
+                    [key_block(buf, block + i, slab) for i in range(pv_blocks)], axis=0
                 )
-
-            acc = lax.fori_loop(
-                0, (tile + 1) * per_tile, add, jnp.zeros((QROWS, head), F32), unroll=4
-            )
-            out[rows, :] = (acc / totals[rows, :]).astype(BF16)
+                acc[rows, :] += jnp.dot(weights[rows, lanes], right, preferred_element_type=F32)
+                return carry
+
+            lax.fori_loop(0, per_tile // pv_blocks, add, 0)
+        total = jnp.sum(totals[...], axis=1, keepdims=True)
+        out[...] = (acc[...] / total).astype(BF16)
 
     return pl.pallas_call(
         kernel,
         out_shape=jax.ShapeDtypeStruct((tokens, head), BF16),
-        in_specs=[pl.BlockSpec(memory_space=VM)] * 3,
+        in_specs=[pl.BlockSpec(memory_space=VM)] * 4,
         out_specs=pl.BlockSpec(memory_space=VM),
         scratch_shapes=[
             pltpu.VMEM((SIDE, SIDE, 2, tokens, head), BF16),
             pltpu.VMEM((tokens, tokens * 2 * SIDE * SIDE), BF16),
             pltpu.VMEM((tokens, TILE), F32),
+            pltpu.VMEM((tokens, TILE), F32),
+            pltpu.VMEM((tokens, head), F32),
+            pltpu.VMEM((n_chan,) + mixed.shape, BF16),
+            pltpu.VMEM((tokens, head), BF16),
         ]
-        + gather_scratch(),
-        compiler_params=pltpu.CompilerParams(collective_id=3, has_side_effects=True),
-    )(queries, keys, values)
+        + gather_scratch()
+        + [
+            pltpu.SemaphoreType.DMA((n_chan,)),
+            pltpu.SemaphoreType.DMA((n_chan,)),
+            pltpu.SemaphoreType.DMA,
+        ],
+        compiler_params=pltpu.CompilerParams(collective_id=2, has_side_effects=True),
+    )(queries, keys, mixed, w_value)
 
 
 def body(n_chan, conv_in, conv_gate, long_filter, skip_gain, queries, keys_in, w_value):
@@ -495,8 +544,7 @@
         (convolved + skip_gain[:, None] * signal_t.astype(F32)) * gate_t.astype(F32)
     ).astype(BF16)
     conv_out = mixed_t.T.reshape(blocks, slab, channels)
-    values = project_values(mixed_t, w_value, n_chan)
-    attended = attend(queries.reshape(tokens, -1), keys, values, slab)
+    attended = attend(queries.reshape(tokens, -1), keys, mixed_t, w_value, slab, n_chan)
     return conv_out, attended.reshape(blocks, slab, -1)
 
 

time: 140 us -> 115 us (0.82)
  Pallas kernels: 125 us -> 101 us
    pallas_call x1 -> x0, Pallas kernels: 21.8 us -> none  [project_values(): pl.pallas_call(kernel, out_shape=jax.ShapeDtypeStruct((tokens, w_value.sh...]
    pallas_call x1, Pallas kernels: 32.1 us -> 24.6 us  [conv_and_keys(): pl.pallas_call(kernel, out_shape=(jax.ShapeDtypeStruct(x.shape, BF16), ja...]
    pallas_call x1, Pallas kernels: 48.4 us -> 51.3 us  [attend(): pl.pallas_call(kernel, out_shape=jax.ShapeDtypeStruct((tokens, head), BF1...]
    pallas_call x2, Pallas kernels: 22.6 us -> 24.9 us  [all_to_all(): pl.pallas_call(kernel, out_shape=jax.ShapeDtypeStruct(blocks.shape, block...]
where the time goes in v2:
time: 115 us
  Pallas kernels  101 us (88%)
  local copies, waits for them, and re-layouts  11.6 us (10%)
  other arithmetic  1.96 us (2%)
    pallas_call x1, Pallas kernels, attend(): pl.pallas_call(kernel, out_shape=jax.ShapeDtypeStruct((tokens, head), BF1...  51.3 us
    pallas_call x2, Pallas kernels, all_to_all(): pl.pallas_call(kernel, out_shape=jax.ShapeDtypeStruct(blocks.shape, block...  24.9 us
    pallas_call x1, Pallas kernels, conv_and_keys(): pl.pallas_call(kernel, out_shape=(jax.ShapeDtypeStruct(x.shape, BF16), ja...  24.6 us

profile of v2, /device:TPU:1, one launch (start us, length us, event | category | flops | bytes accessed | tf_op | source)
XLA Modules:
  0.0 115.1 jit_solution(2432319351303420714)
XLA Ops:
  0.6 1.0 copy.16
  1.7 1.0 convert_element_type.33
  2.6 0.1 copy.17
  2.8 0.2 pad_maximum_fusion
  3.0 0.1 copy.18
  3.1 0.7 reshape.53.src
  3.8 13.1 %shard_map.86 = bf16[32,16,128]{2,1,0:T(8,128)(2,1)} custom-call(bf16[32,16,128]{2,1,0:T(8,128)(2,1)} %reshape.53.src), custom_call_target="tpu_custom_call" | custom-call | tf_op jit(solution)/shard_map/pallas_call | solution.py:83
  16.9 1.2 %copy.19 = bf16[32,16,128]{0,2,1:T(8,128)(2,1)S(1)} copy(bf16[32,16,128]{2,1,0:T(8,128)(2,1)} %shard_map.86) | data formatting | bytes 262144 | tf_op jit(solution)/shard_map/pallas_call | solution.py:83
  18.2 0.3 copy.21
  18.4 0.5 convert_element_type.35
  19.1 0.7 reshape.64.h_ref
  19.8 0.3 copy.20
  20.1 1.0 reshape_squeeze.3.x_ref
  21.0 24.6 %shard_map.87 = (bf16[2,128,128]{2,1,0:T(8,128)(2,1)}, bf16[4,4,2,512,128]{4,3,2,1,0:T(8,128)(2,1)}) custom-call(bf16[2,128,128]{2,1,0:T(8,128)(2,1)} %reshape_squeeze.3.x_ref, f32[2,1,16512]{2,1,0:T(1,128)} %reshape.64.h_ref, bf16[512,128]{1,0:T(8,128)(2,1)} %bitcast.37), custom_call_target="tpu_custom_call" | custom-call | tf_op jit(solution)/shard_map/pallas_call | solution.py:306
  45.7 1.2 %reshape.58 = bf16[2,32,32,16]{3,2,1,0:T(8,128)(2,1)S(1)} reshape(bf16[2,128,128]{2,1,0:T(8,128)(2,1)} %get-tuple-element.4) | data formatting | bytes 131072 | tf_op jit(solution)/shard_map/reshape | solution.py:537
  46.9 0.2 copy.22
  47.1 0.8 copy.23.src
  47.9 11.8 %shard_map.88 = bf16[32,8,128]{2,1,0:T(8,128)(2,1)} custom-call(bf16[32,8,128]{2,1,0:T(8,128)(2,1)} %copy.23.src), custom_call_target="tpu_custom_call" | custom-call | tf_op jit(solution)/shard_map/pallas_call | solution.py:83
  59.7 0.9 reshape.65
  60.7 0.1 copy.24
  60.8 0.7 fusion.m_ref
  61.5 51.3 %shard_map.89 = bf16[512,128]{1,0:T(8,128)(2,1)} custom-call(bf16[512,128]{1,0:T(8,128)(2,1)} %bitcast.34, bf16[4,4,2,512,128]{4,3,2,1,0:T(8,128)(2,1)} %get-tuple-element.5.k_buf, bf16[64,512]{1,0:T(8,128)(2,1)} %fusion.m_ref, bf16[512,128]{1,0:T(8,128)(2,1)} %w_ref.1), custom_call_target="tpu_custom_call" | custom-call | tf_op jit(solution)/shard_map/pallas_call | solution.py:493
  112.8 0.8 copy.25
  113.6 1.6 %copy.27 = bf16[32,16,128]{2,1,0:T(8,128)(2,1)} copy(bf16[32,16,128]{2,1,0:T(8,128)(2,1)} %bitcast.32) | data formatting | bytes 262144
  (11 shorter events, 0.2 us)
Async XLA Ops:
  2.8 57.8 %copy-start.1 = (bf16[32,16,64]{2,1,0:T(8,128)(2,1)S(1)}, bf16[32,16,64]{2,1,0:T(8,128)(2,1)}, u32[]{:S(2)}) copy-start(bf16[32,16,64]{2,1,0:T(8,128)(2,1)} %param.8) | copy-start | bytes 196612
  3.8 57.0 %copy-start.2 = (f32[64]{0:T(128)S(1)}, f32[64]{0:T(128)}, u32[]{:S(2)}) copy-start(f32[64]{0:T(128)} %param.10) | copy-start | bytes 772
  61.5 51.3 %copy-start = (bf16[64,512]{1,0:T(8,128)(2,1)S(1)}, bf16[64,512]{1,0:T(8,128)(2,1)}, u32[]{:S(2)}) copy-start(bf16[64,512]{1,0:T(8,128)(2,1)} %fusion.m_ref) | copy-start | bytes 196612

commit v3 on v2

--- a/solution.py
+++ b/solution.py
@@ -95,7 +95,7 @@
 
 
 SIDE = 4
-COPIES = 26
+COPIES = 28
 
 
 class Gather:
@@ -144,7 +144,7 @@
         return self.buf.at[y, :, core, rows]
 
     def sems(self, half, number):
-        index = half * 13 + number
+        index = half * 14 + number
         return self.send.at[index], self.recv.at[index]
 
     def greet(self):
@@ -161,23 +161,24 @@
         dst = self.one(half, -by) if landing else self.one(half, 0)
         return remote(self.own_ref.at[rows], dst, *self.sems(half, i), self.step(half, 1, by))
 
-    def second(self, half, i, landing=False):
+    def second(self, half, i, part, landing=False):
         by = (1, -1)[i]
-        dst = self.row(half, -by) if landing else self.row(half, 0)
-        return remote(self.row(half, 0), dst, *self.sems(half, 3 + i), self.step(half, 2, by))
+        src = self.row(half, 0, part=part)
+        dst = self.row(half, -by, part=part) if landing else src
+        return remote(src, dst, *self.sems(half, 3 + 2 * i + part), self.step(half, 2, by))
 
     def relay(self, half, i, landing=False):
         by = (1, -1)[i]
         src = self.row(half, -by, part=i)
         dst = self.row(half, 2, part=i) if landing else src
-        return remote(src, dst, *self.sems(half, 5 + i), self.step(half, 2, by))
+        return remote(src, dst, *self.sems(half, 7 + i), self.step(half, 2, by))
 
     def across(self, half, i, landing=False):
         by, part = ((0, None), (-1, None), (1, None), (2, 0), (2, 1))[i]
         src = self.row(half, by, part=part)
         dst = self.row(half, by, core=1 - self.core, part=part) if landing else src
         return remote(
-            src, dst, *self.sems(half, 7 + i), self.at(self.y, self.x, 1 - self.core)
+            src, dst, *self.sems(half, 9 + i), self.at(self.y, self.x, 1 - self.core)
         )
 
     def start(self):
@@ -195,20 +196,23 @@
             for i in range(3):
                 self.first(half, i, True).wait_recv()
             for i in range(2):
-                self.second(half, i).start()
+                self.second(half, i, i).start()
         for half in range(2):
+            for i in range(2):
+                self.second(half, i, 1 - i).start()
             self.across(half, 0).start()
 
     def late(self):
         for i in range(2):
             for half in range(2):
-                self.second(half, i, True).wait_recv()
+                self.second(half, i, i, True).wait_recv()
                 self.relay(half, i).start()
+
+    def last(self):
         for i in range(2):
             for half in range(2):
+                self.second(half, i, 1 - i, True).wait_recv()
                 self.across(half, 1 + i).start()
-
-    def last(self):
         for i in range(2):
             for half in range(2):
                 self.relay(half, i, True).wait_recv()
@@ -222,7 +226,8 @@
             for i in range(3):
                 self.first(half, i).wait_send()
             for i in range(2):
-                self.second(half, i).wait_send()
+                self.second(half, i, 0).wait_send()
+                self.second(half, i, 1).wait_send()
                 self.relay(half, i).wait_send()
             for i in range(5):
                 self.across(half, i).wait_send()
@@ -322,6 +327,8 @@
 
 
 QROWS = 128
+SLICE = 32
+UNROLL = 2
 
 
 def key_block(buf, index, slab):
@@ -398,44 +405,44 @@
         def allowed(tile, block, part):
             return (block - tile * per_tile) * width + part * TILE <= limit
 
-        def edge(tile, block, part, values, other):
-            top = jnp.where(allowed(tile, block, part), values[:QROWS], other)
-            if values.shape[0] == QROWS:
-                return top
-            return jnp.concatenate([top, values[QROWS:]], axis=0)
+        def edge(tile, block, part, start, values, other):
+            if start >= QROWS:
+                return values
+            here = allowed(tile, block, part)[start : start + SLICE]
+            return jnp.where(here, values, other)
 
         def find_best(tile, low, high):
-            rows = pl.ds(tile * QROWS, tokens - tile * QROWS)
-
             def one(block, carry):
                 s = scores(tile, block)
-                top = best[rows, :]
-                for part in range(groups):
-                    piece = s[:, part * TILE : (part + 1) * TILE]
-                    top = jnp.maximum(top, edge(tile, block, part, piece, -1e30))
-                best[rows, :] = top
+                for start in range(0, s.shape[0], SLICE):
+                    rows = pl.ds(tile * QROWS + start, SLICE)
+                    top = best[rows, :]
+                    for part in range(groups):
+                        piece = s[start : start + SLICE, part * TILE : (part + 1) * TILE]
+                        top = jnp.maximum(top, edge(tile, block, part, start, piece, -1e30))
+                    best[rows, :] = top
                 return carry
 
-            lax.fori_loop(tile * per_tile + low, tile * per_tile + high, one, 0)
+            lax.fori_loop(tile * per_tile + low, tile * per_tile + high, one, 0, unroll=UNROLL)
 
         def weigh(tile, low, high):
-            rows = pl.ds(tile * QROWS, tokens - tile * QROWS)
-
             def one(block, carry):
                 s = scores(tile, block)
-                top = best[rows, :]
-                total = totals[rows, :]
-                for part in range(groups):
-                    piece = s[:, part * TILE : (part + 1) * TILE]
-                    w = jnp.exp2((piece - top) * scale)
-                    w = edge(tile, block, part, w, 0.0)
-                    lanes = pl.ds(pl.multiple_of(block * width + part * TILE, TILE), TILE)
-                    weights[rows, lanes] = w.astype(BF16)
-                    total = total + w
-                totals[rows, :] = total
+                for start in range(0, s.shape[0], SLICE):
+                    rows = pl.ds(tile * QROWS + start, SLICE)
+                    top = best[rows, :]
+                    total = totals[rows, :]
+                    for part in range(groups):
+                        piece = s[start : start + SLICE, part * TILE : (part + 1) * TILE]
+                        w = jnp.exp2((piece - top) * scale)
+                        w = edge(tile, block, part, start, w, 0.0)
+                        lanes = pl.ds(pl.multiple_of(block * width + part * TILE, TILE), TILE)
+                        weights[rows, lanes] = w.astype(BF16)
+                        total = total + w
+                    totals[rows, :] = total
                 return carry
 
-            lax.fori_loop(tile * per_tile + low, tile * per_tile + high, one, 0)
+            lax.fori_loop(tile * per_tile + low, tile * per_tile + high, one, 0, unroll=UNROLL)
 
         ring = Ring(n_chan, m_ref, held, ring_send, ring_recv, ring_own)
         gather = Gather(value, buf, send, recv, own)
@@ -486,7 +493,7 @@
                 acc[rows, :] += jnp.dot(weights[rows, lanes], right, preferred_element_type=F32)
                 return carry
 
-            lax.fori_loop(0, per_tile // pv_blocks, add, 0)
+            lax.fori_loop(0, per_tile // pv_blocks, add, 0, unroll=UNROLL)
         total = jnp.sum(totals[...], axis=1, keepdims=True)
         out[...] = (acc[...] / total).astype(BF16)
 

time: 115 us -> 109 us (0.948)
  Pallas kernels: 101 us -> 94.8 us
    pallas_call x1, Pallas kernels: 51.3 us -> 46.2 us  [attend(): pl.pallas_call(kernel, out_shape=jax.ShapeDtypeStruct((tokens, head), BF1...]
where the time goes in v3:
time: 109 us
  Pallas kernels  94.8 us (87%)
  local copies, waits for them, and re-layouts  11.6 us (11%)
  other arithmetic  1.96 us (2%)
    pallas_call x1, Pallas kernels, attend(): pl.pallas_call(kernel, out_shape=jax.ShapeDtypeStruct((tokens, head), BF1...  46.2 us
    pallas_call x2, Pallas kernels, all_to_all(): pl.pallas_call(kernel, out_shape=jax.ShapeDtypeStruct(blocks.shape, block...  24.9 us
    pallas_call x1, Pallas kernels, conv_and_keys(): pl.pallas_call(kernel, out_shape=(jax.ShapeDtypeStruct(x.shape, BF16), ja...  23.8 us

profile of v3, /device:TPU:1, one launch (start us, length us, event | category | flops | bytes accessed | tf_op | source)
XLA Modules:
  0.0 109.1 jit_solution(1662111543264100033)
XLA Ops:
  0.6 1.0 copy.16
  1.7 1.0 convert_element_type.33
  2.6 0.1 copy.17
  2.8 0.2 pad_maximum_fusion
  3.0 0.1 copy.18
  3.1 0.7 reshape.53.src
  3.8 13.1 %shard_map.86 = bf16[32,16,128]{2,1,0:T(8,128)(2,1)} custom-call(bf16[32,16,128]{2,1,0:T(8,128)(2,1)} %reshape.53.src), custom_call_target="tpu_custom_call" | custom-call | tf_op jit(solution)/shard_map/pallas_call | solution.py:83
  16.9 1.2 %copy.19 = bf16[32,16,128]{0,2,1:T(8,128)(2,1)S(1)} copy(bf16[32,16,128]{2,1,0:T(8,128)(2,1)} %shard_map.86) | data formatting | bytes 262144 | tf_op jit(solution)/shard_map/pallas_call | solution.py:83
  18.2 0.3 copy.21
  18.4 0.5 convert_element_type.35
  19.1 0.7 reshape.64.h_ref
  19.8 0.3 copy.20
  20.1 1.0 reshape_squeeze.3.x_ref
  21.0 23.8 %shard_map.87 = (bf16[2,128,128]{2,1,0:T(8,128)(2,1)}, bf16[4,4,2,512,128]{4,3,2,1,0:T(8,128)(2,1)}) custom-call(bf16[2,128,128]{2,1,0:T(8,128)(2,1)} %reshape_squeeze.3.x_ref, f32[2,1,16512]{2,1,0:T(1,128)} %reshape.64.h_ref, bf16[512,128]{1,0:T(8,128)(2,1)} %bitcast.37), custom_call_target="tpu_custom_call" | custom-call | tf_op jit(solution)/shard_map/pallas_call | solution.py:311
  44.8 1.2 %reshape.58 = bf16[2,32,32,16]{3,2,1,0:T(8,128)(2,1)S(1)} reshape(bf16[2,128,128]{2,1,0:T(8,128)(2,1)} %get-tuple-element.4) | data formatting | bytes 131072 | tf_op jit(solution)/shard_map/reshape | solution.py:544
  46.0 0.2 copy.22
  46.2 0.8 copy.23.src
  47.0 11.8 %shard_map.88 = bf16[32,8,128]{2,1,0:T(8,128)(2,1)} custom-call(bf16[32,8,128]{2,1,0:T(8,128)(2,1)} %copy.23.src), custom_call_target="tpu_custom_call" | custom-call | tf_op jit(solution)/shard_map/pallas_call | solution.py:83
  58.8 0.9 reshape.65
  59.7 0.1 copy.24
  59.9 0.7 fusion.m_ref
  60.6 46.2 %shard_map.89 = bf16[512,128]{1,0:T(8,128)(2,1)} custom-call(bf16[512,128]{1,0:T(8,128)(2,1)} %bitcast.34, bf16[4,4,2,512,128]{4,3,2,1,0:T(8,128)(2,1)} %get-tuple-element.5.k_buf, bf16[64,512]{1,0:T(8,128)(2,1)} %fusion.m_ref, bf16[512,128]{1,0:T(8,128)(2,1)} %w_ref.1), custom_call_target="tpu_custom_call" | custom-call | tf_op jit(solution)/shard_map/pallas_call | solution.py:500
  106.8 0.8 copy.25
  107.6 1.6 %copy.27 = bf16[32,16,128]{2,1,0:T(8,128)(2,1)} copy(bf16[32,16,128]{2,1,0:T(8,128)(2,1)} %bitcast.32) | data formatting | bytes 262144
  (11 shorter events, 0.2 us)
Async XLA Ops:
  2.8 56.9 %copy-start.1 = (bf16[32,16,64]{2,1,0:T(8,128)(2,1)S(1)}, bf16[32,16,64]{2,1,0:T(8,128)(2,1)}, u32[]{:S(2)}) copy-start(bf16[32,16,64]{2,1,0:T(8,128)(2,1)} %param.8) | copy-start | bytes 196612
  3.8 56.0 %copy-start.2 = (f32[64]{0:T(128)S(1)}, f32[64]{0:T(128)}, u32[]{:S(2)}) copy-start(f32[64]{0:T(128)} %param.10) | copy-start | bytes 772
  60.6 46.2 %copy-start = (bf16[64,512]{1,0:T(8,128)(2,1)S(1)}, bf16[64,512]{1,0:T(8,128)(2,1)}, u32[]{:S(2)}) copy-start(bf16[64,512]{1,0:T(8,128)(2,1)} %fusion.m_ref) | copy-start | bytes 196612

commit v4 on v3

--- a/solution.py
+++ b/solution.py
@@ -34,73 +34,103 @@
     )
 
 
-def exchange_kernel(n, along_seq, spread, src, dst, send, recv, own):
+def exchange_kernel(n, src, dst, send, recv, own, beside=None):
     seq = lax.axis_index("seq")
     chan = lax.axis_index("chan")
-    me = seq if along_seq else chan
+    me = seq
 
     def peer(step):
         other = lax.rem(me + step, n)
-        return other, (device_at(other, chan) if along_seq else device_at(seq, other))
+        return other, device_at(other, chan)
 
     def greet(step, carry):
         signal(peer(step)[1])
         return carry
 
     lax.fori_loop(1, n, greet, 0)
-    local = pltpu.make_async_copy(src if spread else src.at[me], dst.at[me], own)
+    local = pltpu.make_async_copy(src.at[me], dst.at[me], own)
     local.start()
     pl.semaphore_wait(pltpu.get_barrier_semaphore(), n - 1)
 
     def post(step, carry):
         other, target = peer(step)
-        remote(
-            src if spread else src.at[other], dst.at[me], send.at[step], recv.at[step], target
-        ).start()
+        remote(src.at[other], dst.at[me], send.at[step], recv.at[step], target).start()
         return carry
 
     lax.fori_loop(1, n, post, 0)
+    if beside is not None:
+        beside.start()
 
     def finish(step, carry):
         other, target = peer(step)
         back = lax.rem(me + n - step, n)
-        done = remote(
-            src if spread else src.at[other], dst.at[back], send.at[step], recv.at[step], target
-        )
-        done.wait()
+        remote(src.at[other], dst.at[back], send.at[step], recv.at[step], target).wait()
         return carry
 
     lax.fori_loop(1, n, finish, 0)
     local.wait()
+    if beside is not None:
+        beside.end()
+
+
+def exchange_scratch(n):
+    return [
+        pltpu.SemaphoreType.DMA((n,)),
+        pltpu.SemaphoreType.DMA((n,)),
+        pltpu.SemaphoreType.DMA,
+    ]
 
 
 def all_to_all(blocks, collective):
     n = blocks.shape[0]
 
     def kernel(src, dst, send, recv, own):
-        exchange_kernel(n, True, False, src, dst, send, recv, own)
+        exchange_kernel(n, src, dst, send, recv, own)
 
     return pl.pallas_call(
         kernel,
         out_shape=jax.ShapeDtypeStruct(blocks.shape, blocks.dtype),
         in_specs=[pl.BlockSpec(memory_space=VM)],
         out_specs=pl.BlockSpec(memory_space=VM),
-        scratch_shapes=[
-            pltpu.SemaphoreType.DMA((n,)),
-            pltpu.SemaphoreType.DMA((n,)),
-            pltpu.SemaphoreType.DMA,
-        ],
+        scratch_shapes=exchange_scratch(n),
         compiler_params=pltpu.CompilerParams(collective_id=collective, has_side_effects=True),
     )(blocks)
 
 
+def exchange_and_rows(blocks, keys):
+    n = blocks.shape[0]
+    tokens, head = keys.shape
+
+    def kernel(src, k_ref, dst, rows, send, recv, own, row_send, row_recv, row_own):
+        beside = FirstRows(k_ref, rows, row_send, row_recv, row_own)
+        exchange_kernel(n, src, dst, send, recv, own, beside)
+
+    return pl.pallas_call(
+        kernel,
+        out_shape=(
+            jax.ShapeDtypeStruct(blocks.shape, blocks.dtype),
+            jax.ShapeDtypeStruct((2, SIDE, tokens // 2, head), BF16),
+        ),
+        in_specs=[pl.BlockSpec(memory_space=VM)] * 2,
+        out_specs=(pl.BlockSpec(memory_space=VM),) * 2,
+        scratch_shapes=exchange_scratch(n)
+        + [
+            pltpu.SemaphoreType.DMA((6,)),
+            pltpu.SemaphoreType.DMA((6,)),
+            pltpu.SemaphoreType.DMA((2,)),
+        ],
+        compiler_params=pltpu.CompilerParams(collective_id=0, has_side_effects=True),
+    )(blocks, keys)
+
+
 SIDE = 4
 COPIES = 28
 
 
 class Gather:
-    def __init__(self, own_ref, buf, send, recv, own_sem):
+    def __init__(self, own_ref, buf, send, recv, own_sem, rows=None):
         seq = lax.axis_index("seq")
+        self.rows = rows
         self.chan = lax.axis_index("chan")
         self.own_ref, self.buf, self.send, self.recv, self.own_sem = (
             own_ref, buf, send, recv, own_sem
@@ -108,7 +138,7 @@
         self.core = lax.rem(seq, 2)
         self.x = lax.rem(seq // 2, SIDE)
         self.y = seq // (2 * SIDE)
-        self.half = own_ref.shape[0] // 2
+        self.half = buf.shape[3] // 2
 
     def at(self, y, x, core):
         return device_at((y * SIDE + x) * 2 + core, self.chan)
@@ -147,12 +177,20 @@
         index = half * 14 + number
         return self.send.at[index], self.recv.at[index]
 
+    def held(self, half, part=None):
+        if self.rows is None:
+            return self.row(half, 0, part=part)
+        if part is None:
+            return self.rows.at[half]
+        return self.rows.at[half, :, pl.ds(part * (self.half // 2), self.half // 2)]
+
     def greet(self):
-        for by in (1, 2, 3):
+        places = (1, 2, 3) if self.rows is None else (1, 3)
+        for by in places:
             signal(self.step(0, 1, by))
             signal(self.step(1, 1, by))
         signal(self.at(self.y, self.x, 1 - self.core))
-        return 7
+        return 2 * len(places) + 1
 
 
     def first(self, half, i, landing=False):
@@ -163,9 +201,8 @@
 
     def second(self, half, i, part, landing=False):
         by = (1, -1)[i]
-        src = self.row(half, 0, part=part)
-        dst = self.row(half, -by, part=part) if landing else src
-        return remote(src, dst, *self.sems(half, 3 + 2 * i + part), self.step(half, 2, by))
+        dst = self.row(half, -by if landing else 0, part=part)
+        return remote(self.held(half, part), dst, *self.sems(half, 3 + 2 * i + part), self.step(half, 2, by))
 
     def relay(self, half, i, landing=False):
         by = (1, -1)[i]
@@ -175,26 +212,40 @@
 
     def across(self, half, i, landing=False):
         by, part = ((0, None), (-1, None), (1, None), (2, 0), (2, 1))[i]
-        src = self.row(half, by, part=part)
-        dst = self.row(half, by, core=1 - self.core, part=part) if landing else src
+        src = self.held(half) if i == 0 else self.row(half, by, part=part)
+        dst = self.row(half, by, core=1 - self.core if landing else self.core, part=part)
         return remote(
             src, dst, *self.sems(half, 9 + i), self.at(self.y, self.x, 1 - self.core)
         )
 
     def start(self):
-        self.local = pltpu.make_async_copy(
-            self.own_ref, self.buf.at[self.y, self.x, self.core], self.own_sem
+        if self.rows is not None:
+            self.local = [
+                pltpu.make_async_copy(self.held(half), self.row(half, 0), self.own_sem.at[half])
+                for half in range(2)
+            ]
+            for copy in self.local:
+                copy.start()
+            self.post()
+            return
+        copy = pltpu.make_async_copy(
+            self.own_ref, self.buf.at[self.y, self.x, self.core], self.own_sem.at[0]
         )
-        self.local.start()
+        copy.start()
+        self.local = [copy]
         for i in range(3):
             for half in range(2):
                 self.first(half, i).start()
 
     def middle(self):
-        self.local.wait()
+        self.local.pop().wait()
         for half in range(2):
             for i in range(3):
                 self.first(half, i, True).wait_recv()
+        self.post()
+
+    def post(self):
+        for half in range(2):
             for i in range(2):
                 self.second(half, i, i).start()
         for half in range(2):
@@ -203,28 +254,32 @@
             self.across(half, 0).start()
 
     def late(self):
-        for i in range(2):
-            for half in range(2):
+        for half in range(2):
+            for i in range(2):
                 self.second(half, i, i, True).wait_recv()
                 self.relay(half, i).start()
 
     def last(self):
-        for i in range(2):
-            for half in range(2):
+        for half in range(2):
+            for i in range(2):
                 self.second(half, i, 1 - i, True).wait_recv()
                 self.across(half, 1 + i).start()
-        for i in range(2):
-            for half in range(2):
+        for half in range(2):
+            for i in range(2):
                 self.relay(half, i, True).wait_recv()
                 self.across(half, 3 + i).start()
 
+    def arrived(self, half):
+        for i in range(5):
+            self.across(half, i, True).wait_recv()
+
     def end(self):
-        for half in range(2):
-            for i in range(5):
-                self.across(half, i, True).wait_recv()
+        for copy in self.local:
+            copy.wait()
         for half in range(2):
             for i in range(3):
-                self.first(half, i).wait_send()
+                if self.rows is None:
+                    self.first(half, i).wait_send()
             for i in range(2):
                 self.second(half, i, 0).wait_send()
                 self.second(half, i, 1).wait_send()
@@ -233,11 +288,53 @@
                 self.across(half, i).wait_send()
 
 
+class FirstRows(Gather):
+    def __init__(self, own_ref, rows, send, recv, own_sem):
+        seq = lax.axis_index("seq")
+        self.chan = lax.axis_index("chan")
+        self.own_ref, self.rows, self.send, self.recv, self.own_sem = (
+            own_ref, rows, send, recv, own_sem
+        )
+        self.core = lax.rem(seq, 2)
+        self.x = lax.rem(seq // 2, SIDE)
+        self.y = seq // (2 * SIDE)
+        self.half = own_ref.shape[0] // 2
+
+    def first(self, half, i, landing=False):
+        by = (1, -1, 2)[i]
+        place = self.x if half == 0 else self.y
+        if landing:
+            place = lax.rem(place - by + SIDE, SIDE)
+        src = self.own_ref.at[pl.ds(half * self.half, self.half)]
+        index = half * 3 + i
+        return remote(
+            src, self.rows.at[half, place], self.send.at[index], self.recv.at[index],
+            self.step(half, 1, by),
+        )
+
+    def local(self, half):
+        src = self.own_ref.at[pl.ds(half * self.half, self.half)]
+        place = self.x if half == 0 else self.y
+        return pltpu.make_async_copy(src, self.rows.at[half, place], self.own_sem.at[half])
+
+    def start(self):
+        for half in range(2):
+            for i in range(3):
+                self.first(half, i).start()
+            self.local(half).start()
+
+    def end(self):
+        for half in range(2):
+            for i in range(3):
+                self.first(half, i, True).wait()
+            self.local(half).wait()
+
+
 def gather_scratch():
     return [
         pltpu.SemaphoreType.DMA((COPIES,)),
         pltpu.SemaphoreType.DMA((COPIES,)),
-        pltpu.SemaphoreType.DMA,
+        pltpu.SemaphoreType.DMA((2,)),
     ]
 
 
@@ -289,14 +386,14 @@
         total[pl.ds(GROUP * g, rows), :] += acc
 
 
-def conv_and_keys(x, h, keys):
-    tokens, head = keys.shape
+def conv_and_keys(x, h, rows):
+    tokens, head = 2 * rows.shape[2], rows.shape[3]
 
     def kernel(x_ref, h_ref, k_ref, y_ref, buf, base, shifted, total, send, recv, own):
-        gather = Gather(k_ref, buf, send, recv, own)
+        gather = Gather(None, buf, send, recv, own, k_ref)
         pl.semaphore_wait(pltpu.get_barrier_semaphore(), gather.greet())
         gather.start()
-        stages = {(0, 1): gather.middle, (0, 7): gather.late, (1, 1): gather.last}
+        stages = {(0, 3): gather.late, (1, 0): gather.last}
         for ch in range(x_ref.shape[0]):
             spread_taps(h_ref, base, ch)
             spread_signal(x_ref, shifted, ch)
@@ -305,6 +402,8 @@
                 if (ch, g) in stages:
                     stages[ch, g]()
             y_ref[ch] = total[...].astype(BF16)
+        for half in range(2):
+            gather.arrived(half)
         gather.end()
 
     blocks = x.shape[1]
@@ -323,7 +422,7 @@
         ]
         + gather_scratch(),
         compiler_params=pltpu.CompilerParams(collective_id=1, has_side_effects=True),
-    )(x, h, keys)
+    )(x, h, rows)
 
 
 QROWS = 128
@@ -477,11 +576,13 @@
         weigh(0, 0, 4)
         gather.late()
         weigh(0, 4, 8)
+        acc[...] = jnp.zeros(acc.shape, F32)
         gather.last()
-        gather.end()
-
-        acc[...] = jnp.zeros(acc.shape, F32)
         for tile in range(tokens // QROWS):
+            if tile == 0:
+                gather.arrived(0)
+            if 2 * tile * QROWS == tokens:
+                gather.arrived(1)
             rows = pl.ds(tile * QROWS, tokens - tile * QROWS)
 
             def add(step, carry, rows=rows, tile=tile):
@@ -494,6 +595,7 @@
                 return carry
 
             lax.fori_loop(0, per_tile // pv_blocks, add, 0, unroll=UNROLL)
+        gather.end()
         total = jnp.sum(totals[...], axis=1, keepdims=True)
         out[...] = (acc[...] / total).astype(BF16)
 
@@ -533,13 +635,13 @@
     packed = jnp.stack(
         [signal_t.reshape(n_seq, each, tokens), taps_t.reshape(n_seq, each, tokens)], axis=1
     ).reshape(n_seq, 2 * each * lines, TILE)
-    got = all_to_all(packed, 0)
+    got, rows = exchange_and_rows(packed, keys_in.reshape(tokens, -1))
     whole = (
         got.reshape(n_seq, 2, each, blocks, slab).transpose(1, 2, 3, 0, 4).reshape(2, each, length)
     )
     x = whole[0].reshape(each, length // TILE, TILE)
     h = jnp.pad(whole[1].astype(F32), ((0, 0), (TILE, 0))).reshape(each, 1, length + TILE)
-    y, keys = conv_and_keys(x, h, keys_in.reshape(tokens, -1))
+    y, keys = conv_and_keys(x, h, rows)
     back = (
         y.reshape(each, blocks, n_seq, slab)
         .transpose(2, 0, 1, 3)

time: 109 us -> 106 us (0.972)
  Pallas kernels: 94.8 us -> 91.3 us
    pallas_call x0 -> x1, Pallas kernels: none -> 15.5 us  [exchange_and_rows(): pl.pallas_call(kernel, out_shape=(jax.ShapeDtypeStruct(blocks.shape, bloc...]
    pallas_call x2 -> x1, Pallas kernels: 24.9 us -> 11.6 us  [all_to_all(): pl.pallas_call(kernel, out_shape=jax.ShapeDtypeStruct(blocks.shape, block...]
    pallas_call x1, Pallas kernels: 23.8 us -> 19.1 us  [conv_and_keys(): pl.pallas_call(kernel, out_shape=(jax.ShapeDtypeStruct(x.shape, BF16), ja...]
    pallas_call x1, Pallas kernels: 46.2 us -> 45 us  [attend(): pl.pallas_call(kernel, out_shape=jax.ShapeDtypeStruct((tokens, head), BF1...]
where the time goes in v4:
time: 106 us
  Pallas kernels  91.3 us (86%)
  local copies, waits for them, and re-layouts  11.6 us (11%)
  other arithmetic  1.96 us (2%)
    pallas_call x1, Pallas kernels, attend(): pl.pallas_call(kernel, out_shape=jax.ShapeDtypeStruct((tokens, head), BF1...  45 us
    pallas_call x1, Pallas kernels, conv_and_keys(): pl.pallas_call(kernel, out_shape=(jax.ShapeDtypeStruct(x.shape, BF16), ja...  19.1 us
    pallas_call x1, Pallas kernels, exchange_and_rows(): pl.pallas_call(kernel, out_shape=(jax.ShapeDtypeStruct(blocks.shape, bloc...  15.5 us
    pallas_call x1, Pallas kernels, all_to_all(): pl.pallas_call(kernel, out_shape=jax.ShapeDtypeStruct(blocks.shape, block...  11.6 us

profile of v4, /device:TPU:1, one launch (start us, length us, event | category | flops | bytes accessed | tf_op | source)
XLA Modules:
  0.0 105.6 jit_solution(16028024435528081881)
XLA Ops:
  0.6 1.0 copy.16
  1.7 1.0 convert_element_type.33
  2.6 0.1 copy.17
  2.8 0.2 pad_maximum_fusion
  3.0 0.1 copy.18
  3.1 0.7 reshape.53.src
  3.8 15.5 %shard_map.86 = (bf16[32,16,128]{2,1,0:T(8,128)(2,1)}, bf16[2,4,256,128]{3,2,1,0:T(8,128)(2,1)}) custom-call(bf16[32,16,128]{2,1,0:T(8,128)(2,1)} %reshape.53.src, bf16[512,128]{1,0:T(8,128)(2,1)} %bitcast.37), custom_call_target="tpu_custom_call" | custom-call | tf_op jit(solution)/shard_map/pallas_call | solution.py:108
  19.3 1.2 %copy.19 = bf16[32,16,128]{0,2,1:T(8,128)(2,1)S(1)} copy(bf16[32,16,128]{2,1,0:T(8,128)(2,1)} %get-tuple-element.6) | data formatting | bytes 262144 | tf_op jit(solution)/shard_map/pallas_call | solution.py:108
  20.6 0.3 copy.21
  20.9 0.5 convert_element_type.35
  21.5 0.7 reshape.64.h_ref
  22.2 0.3 copy.20
  22.5 1.0 reshape_squeeze.3.x_ref
  23.5 19.1 %shard_map.87 = (bf16[2,128,128]{2,1,0:T(8,128)(2,1)}, bf16[4,4,2,512,128]{4,3,2,1,0:T(8,128)(2,1)}) custom-call(bf16[2,128,128]{2,1,0:T(8,128)(2,1)} %reshape_squeeze.3.x_ref, f32[2,1,16512]{2,1,0:T(1,128)} %reshape.64.h_ref, bf16[2,4,256,128]{3,2,1,0:T(8,128)(2,1)} %get-tuple-element.7.k_ref), custom_call_target="tpu_custom_call" | custom-call | tf_op jit(solution)/shard_map/pallas_call | solution.py:410
  42.6 1.2 %reshape.58 = bf16[2,32,32,16]{3,2,1,0:T(8,128)(2,1)S(1)} reshape(bf16[2,128,128]{2,1,0:T(8,128)(2,1)} %get-tuple-element.8) | data formatting | bytes 131072 | tf_op jit(solution)/shard_map/reshape | solution.py:646
  43.8 0.2 copy.22
  44.0 0.8 copy.23.src
  44.8 11.6 %shard_map.88 = bf16[32,8,128]{2,1,0:T(8,128)(2,1)} custom-call(bf16[32,8,128]{2,1,0:T(8,128)(2,1)} %copy.23.src), custom_call_target="tpu_custom_call" | custom-call | tf_op jit(solution)/shard_map/pallas_call | solution.py:90
  56.4 0.9 reshape.65
  57.4 0.1 copy.24
  57.5 0.7 fusion.m_ref
  58.2 45.0 %shard_map.89 = bf16[512,128]{1,0:T(8,128)(2,1)} custom-call(bf16[512,128]{1,0:T(8,128)(2,1)} %bitcast.34, bf16[4,4,2,512,128]{4,3,2,1,0:T(8,128)(2,1)} %get-tuple-element.9.k_buf, bf16[64,512]{1,0:T(8,128)(2,1)} %fusion.m_ref, bf16[512,128]{1,0:T(8,128)(2,1)} %w_ref.1), custom_call_target="tpu_custom_call" | custom-call | tf_op jit(solution)/shard_map/pallas_call | solution.py:602
  103.3 0.8 copy.25
  104.0 1.6 %copy.27 = bf16[32,16,128]{2,1,0:T(8,128)(2,1)} copy(bf16[32,16,128]{2,1,0:T(8,128)(2,1)} %bitcast.32) | data formatting | bytes 262144
  (11 shorter events, 0.2 us)
Async XLA Ops:
  3.0 54.4 %copy-start.1 = (bf16[32,16,64]{2,1,0:T(8,128)(2,1)S(1)}, bf16[32,16,64]{2,1,0:T(8,128)(2,1)}, u32[]{:S(2)}) copy-start(bf16[32,16,64]{2,1,0:T(8,128)(2,1)} %param.8) | copy-start | bytes 196612
  19.3 38.2 %copy-start.2 = (f32[64]{0:T(128)S(1)}, f32[64]{0:T(128)}, u32[]{:S(2)}) copy-start(f32[64]{0:T(128)} %param.10) | copy-start | bytes 772
  58.2 45.0 %copy-start = (bf16[64,512]{1,0:T(8,128)(2,1)S(1)}, bf16[64,512]{1,0:T(8,128)(2,1)}, u32[]{:S(2)}) copy-start(bf16[64,512]{1,0:T(8,128)(2,1)} %fusion.m_ref) | copy-start | bytes 196612

commit v5 on v4

--- a/solution.py
+++ b/solution.py
@@ -273,9 +273,12 @@
         for i in range(5):
             self.across(half, i, True).wait_recv()
 
+    def placed(self):
+        while self.local:
+            self.local.pop().wait()
+
     def end(self):
-        for copy in self.local:
-            copy.wait()
+        self.placed()
         for half in range(2):
             for i in range(3):
                 if self.rows is None:
@@ -389,8 +392,16 @@
 def conv_and_keys(x, h, rows):
     tokens, head = 2 * rows.shape[2], rows.shape[3]
 
-    def kernel(x_ref, h_ref, k_ref, y_ref, buf, base, shifted, total, send, recv, own):
+    def kernel(
+        x_ref, h_ref, k_ref, y_ref, keys_out, buf, base, shifted, total, send, recv, own, away
+    ):
         gather = Gather(None, buf, send, recv, own, k_ref)
+
+        def write_out(index, core):
+            return pltpu.make_async_copy(
+                buf.at[:, :, core], keys_out.at[:, :, core], away.at[index]
+            )
+
         pl.semaphore_wait(pltpu.get_barrier_semaphore(), gather.greet())
         gather.start()
         stages = {(0, 3): gather.late, (1, 0): gather.last}
@@ -401,10 +412,16 @@
                 convolve_group(base, shifted, total, g, x_ref.shape[1])
                 if (ch, g) in stages:
                     stages[ch, g]()
+                if (ch, g) == (1, 0):
+                    gather.placed()
+                    write_out(0, gather.core).start()
             y_ref[ch] = total[...].astype(BF16)
         for half in range(2):
             gather.arrived(half)
+        write_out(1, 1 - gather.core).start()
         gather.end()
+        write_out(0, gather.core).wait()
+        write_out(1, 1 - gather.core).wait()
 
     blocks = x.shape[1]
     return pl.pallas_call(
@@ -414,13 +431,15 @@
             jax.ShapeDtypeStruct((SIDE, SIDE, 2, tokens, head), BF16),
         ),
         in_specs=[pl.BlockSpec(memory_space=VM)] * 3,
-        out_specs=(pl.BlockSpec(memory_space=VM),) * 2,
+        out_specs=(pl.BlockSpec(memory_space=VM), pl.BlockSpec(memory_space=pl.ANY)),
         scratch_shapes=[
+            pltpu.VMEM((SIDE, SIDE, 2, tokens, head), BF16),
             pltpu.VMEM((8, h.shape[2]), F32),
             pltpu.VMEM((GROUP // AT_ONCE, blocks, AT_ONCE * TILE), BF16),
             pltpu.VMEM((blocks, TILE), F32),
         ]
-        + gather_scratch(),
+        + gather_scratch()
+        + [pltpu.SemaphoreType.DMA((2,))],
         compiler_params=pltpu.CompilerParams(collective_id=1, has_side_effects=True),
     )(x, h, rows)
 
@@ -486,8 +505,8 @@
     pv_blocks = 2
 
     def kernel(
-        q_ref, k_buf, m_ref, w_ref, out, buf, weights, best, totals, acc, held, value,
-        send, recv, own, ring_send, ring_recv, ring_own,
+        q_ref, k_far, m_ref, w_ref, out, k_buf, buf, weights, best, totals, acc, held, value,
+        send, recv, own, ring_send, ring_recv, ring_own, fetched,
     ):
         first_row = lax.axis_index("seq") * slab
         row = lax.broadcasted_iota(jnp.int32, (QROWS, TILE), 0)
@@ -543,6 +562,8 @@
 
             lax.fori_loop(tile * per_tile + low, tile * per_tile + high, one, 0, unroll=UNROLL)
 
+        fetch = pltpu.make_async_copy(k_far, k_buf, fetched)
+        fetch.start()
         ring = Ring(n_chan, m_ref, held, ring_send, ring_recv, ring_own)
         gather = Gather(value, buf, send, recv, own)
         greeted = ring.greet() + gather.greet()
@@ -551,6 +572,7 @@
         ring.start(1)
         best[...] = jnp.full(best.shape, -1e30, F32)
         totals[...] = jnp.zeros(totals.shape, F32)
+        fetch.wait()
         find_best(0, 0, 4)
         ring.start(2)
         find_best(0, 4, 8)
@@ -567,8 +589,9 @@
             (((0,), (0,)), ((), ())),
             preferred_element_type=F32,
         ).astype(BF16)
-        weigh(3, 0, 8)
+        weigh(3, 0, 2)
         gather.start()
+        weigh(3, 2, 8)
         weigh(2, 0, 8)
         weigh(1, 0, 4)
         gather.middle()
@@ -602,9 +625,10 @@
     return pl.pallas_call(
         kernel,
         out_shape=jax.ShapeDtypeStruct((tokens, head), BF16),
-        in_specs=[pl.BlockSpec(memory_space=VM)] * 4,
+        in_specs=[pl.BlockSpec(memory_space=pl.ANY if i == 1 else VM) for i in range(4)],
         out_specs=pl.BlockSpec(memory_space=VM),
         scratch_shapes=[
+            pltpu.VMEM((SIDE, SIDE, 2, tokens, head), BF16),
             pltpu.VMEM((SIDE, SIDE, 2, tokens, head), BF16),
             pltpu.VMEM((tokens, tokens * 2 * SIDE * SIDE), BF16),
             pltpu.VMEM((tokens, TILE), F32),
@@ -617,6 +641,7 @@
         + [
             pltpu.SemaphoreType.DMA((n_chan,)),
             pltpu.SemaphoreType.DMA((n_chan,)),
+            pltpu.SemaphoreType.DMA,
             pltpu.SemaphoreType.DMA,
         ],
         compiler_params=pltpu.CompilerParams(collective_id=2, has_side_effects=True),

time: 106 us -> 104 us (0.981)
  Pallas kernels: 91.3 us -> 88.9 us
    pallas_call x1, Pallas kernels: 45 us -> 42.7 us  [attend(): pl.pallas_call(kernel, out_shape=jax.ShapeDtypeStruct((tokens, head), BF1...]
where the time goes in v5:
time: 104 us; the launch traced here: 103 us
  Pallas kernels  88.9 us (85%)
  local copies, waits for them, and re-layouts  11.6 us (11%)
  other arithmetic  1.96 us (2%)
    pallas_call x1, Pallas kernels, attend(): pl.pallas_call(kernel, out_shape=jax.ShapeDtypeStruct((tokens, head), BF1...  42.7 us
    pallas_call x1, Pallas kernels, conv_and_keys(): pl.pallas_call(kernel, out_shape=(jax.ShapeDtypeStruct(x.shape, BF16), ja...  19.1 us
    pallas_call x1, Pallas kernels, exchange_and_rows(): pl.pallas_call(kernel, out_shape=(jax.ShapeDtypeStruct(blocks.shape, bloc...  15.5 us
    pallas_call x1, Pallas kernels, all_to_all(): pl.pallas_call(kernel, out_shape=jax.ShapeDtypeStruct(blocks.shape, block...  11.7 us

profile of v5, /device:TPU:1, one launch (start us, length us, event | category | flops | bytes accessed | tf_op | source)
XLA Modules:
  0.0 103.2 jit_solution(5941526628961630970)
XLA Ops:
  0.6 1.0 copy.16
  1.7 1.0 convert_element_type.33
  2.6 0.1 copy.17
  2.8 0.2 pad_maximum_fusion
  3.0 0.1 copy.18
  3.1 0.7 reshape.53.src
  3.8 15.5 %shard_map.86 = (bf16[32,16,128]{2,1,0:T(8,128)(2,1)}, bf16[2,4,256,128]{3,2,1,0:T(8,128)(2,1)}) custom-call(bf16[32,16,128]{2,1,0:T(8,128)(2,1)} %reshape.53.src, bf16[512,128]{1,0:T(8,128)(2,1)} %bitcast.37), custom_call_target="tpu_custom_call" | custom-call | tf_op jit(solution)/shard_map/pallas_call | solution.py:108
  19.3 1.2 %copy.19 = bf16[32,16,128]{0,2,1:T(8,128)(2,1)S(1)} copy(bf16[32,16,128]{2,1,0:T(8,128)(2,1)} %get-tuple-element.6) | data formatting | bytes 262144 | tf_op jit(solution)/shard_map/pallas_call | solution.py:108
  20.6 0.3 copy.21
  20.9 0.5 convert_element_type.35
  21.5 0.7 reshape.64.h_ref
  22.2 0.3 copy.20
  22.5 1.0 reshape_squeeze.3.x_ref
  23.5 19.1 %shard_map.87 = (bf16[2,128,128]{2,1,0:T(8,128)(2,1)}, bf16[4,4,2,512,128]{4,3,2,1,0:T(8,128)(2,1)}) custom-call(bf16[2,128,128]{2,1,0:T(8,128)(2,1)} %reshape_squeeze.3.x_ref, f32[2,1,16512]{2,1,0:T(1,128)} %reshape.64.h_ref, bf16[2,4,256,128]{3,2,1,0:T(8,128)(2,1)} %get-tuple-element.7.k_ref), custom_call_target="tpu_custom_call" | custom-call | tf_op jit(solution)/shard_map/pallas_call | solution.py:427
  42.5 1.2 %reshape.58 = bf16[2,32,32,16]{3,2,1,0:T(8,128)(2,1)S(1)} reshape(bf16[2,128,128]{2,1,0:T(8,128)(2,1)} %get-tuple-element.8) | data formatting | bytes 131072 | tf_op jit(solution)/shard_map/reshape | solution.py:671
  43.7 0.2 copy.22
  44.0 0.8 copy.23.src
  44.7 11.7 %shard_map.88 = bf16[32,8,128]{2,1,0:T(8,128)(2,1)} custom-call(bf16[32,8,128]{2,1,0:T(8,128)(2,1)} %copy.23.src), custom_call_target="tpu_custom_call" | custom-call | tf_op jit(solution)/shard_map/pallas_call | solution.py:90
  56.4 0.9 reshape.65
  57.3 0.1 copy.24
  57.5 0.7 fusion.m_ref
  58.2 42.7 %shard_map.89 = bf16[512,128]{1,0:T(8,128)(2,1)} custom-call(bf16[512,128]{1,0:T(8,128)(2,1)} %bitcast.34, bf16[4,4,2,512,128]{4,3,2,1,0:T(8,128)(2,1)} %get-tuple-element.9.k_far, bf16[64,512]{1,0:T(8,128)(2,1)} %fusion.m_ref, bf16[512,128]{1,0:T(8,128)(2,1)} %w_ref.1), custom_call_target="tpu_custom_call" | custom-call | tf_op jit(solution)/shard_map/pallas_call | solution.py:625
  100.9 0.8 copy.25
  101.7 1.6 %copy.27 = bf16[32,16,128]{2,1,0:T(8,128)(2,1)} copy(bf16[32,16,128]{2,1,0:T(8,128)(2,1)} %bitcast.32) | data formatting | bytes 262144
  (11 shorter events, 0.2 us)
Async XLA Ops:
  3.0 54.3 %copy-start.1 = (bf16[32,16,64]{2,1,0:T(8,128)(2,1)S(1)}, bf16[32,16,64]{2,1,0:T(8,128)(2,1)}, u32[]{:S(2)}) copy-start(bf16[32,16,64]{2,1,0:T(8,128)(2,1)} %param.8) | copy-start | bytes 196612
  19.3 38.1 %copy-start.2 = (f32[64]{0:T(128)S(1)}, f32[64]{0:T(128)}, u32[]{:S(2)}) copy-start(f32[64]{0:T(128)} %param.10) | copy-start | bytes 772
  58.2 42.7 %copy-start = (bf16[64,512]{1,0:T(8,128)(2,1)S(1)}, bf16[64,512]{1,0:T(8,128)(2,1)}, u32[]{:S(2)}) copy-start(bf16[64,512]{1,0:T(8,128)(2,1)} %fusion.m_ref) | copy-start | bytes 196612

commit v6 on v5

--- a/solution.py
+++ b/solution.py
@@ -404,7 +404,7 @@
 
         pl.semaphore_wait(pltpu.get_barrier_semaphore(), gather.greet())
         gather.start()
-        stages = {(0, 3): gather.late, (1, 0): gather.last}
+        stages = {(0, 3): gather.late, (1, 2): gather.last}
         for ch in range(x_ref.shape[0]):
             spread_taps(h_ref, base, ch)
             spread_signal(x_ref, shifted, ch)
@@ -412,7 +412,7 @@
                 convolve_group(base, shifted, total, g, x_ref.shape[1])
                 if (ch, g) in stages:
                     stages[ch, g]()
-                if (ch, g) == (1, 0):
+                if (ch, g) == (1, 2):
                     gather.placed()
                     write_out(0, gather.core).start()
             y_ref[ch] = total[...].astype(BF16)
@@ -593,12 +593,10 @@
         gather.start()
         weigh(3, 2, 8)
         weigh(2, 0, 8)
-        weigh(1, 0, 4)
         gather.middle()
-        weigh(1, 4, 8)
-        weigh(0, 0, 4)
+        weigh(1, 0, 8)
         gather.late()
-        weigh(0, 4, 8)
+        weigh(0, 0, 8)
         acc[...] = jnp.zeros(acc.shape, F32)
         gather.last()
         for tile in range(tokens // QROWS):

time: 104 us -> 103 us (level)
    pallas_call x1, Pallas kernels: 11.7 us -> 9.65 us  [all_to_all(): pl.pallas_call(kernel, out_shape=jax.ShapeDtypeStruct(blocks.shape, block...]
where the time goes in v6:
time: 103 us
  Pallas kernels  88.4 us (86%)
  local copies, waits for them, and re-layouts  11.6 us (11%)
  other arithmetic  1.96 us (2%)
    pallas_call x1, Pallas kernels, attend(): pl.pallas_call(kernel, out_shape=jax.ShapeDtypeStruct((tokens, head), BF1...  43.3 us
    pallas_call x1, Pallas kernels, conv_and_keys(): pl.pallas_call(kernel, out_shape=(jax.ShapeDtypeStruct(x.shape, BF16), ja...  19.9 us
    pallas_call x1, Pallas kernels, exchange_and_rows(): pl.pallas_call(kernel, out_shape=(jax.ShapeDtypeStruct(blocks.shape, bloc...  15.5 us
    pallas_call x1, Pallas kernels, all_to_all(): pl.pallas_call(kernel, out_shape=jax.ShapeDtypeStruct(blocks.shape, block...  9.65 us

profile of v6, /device:TPU:1, one launch (start us, length us, event | category | flops | bytes accessed | tf_op | source)
XLA Modules:
  0.0 102.7 jit_solution(1547044069015369054)
XLA Ops:
  0.6 1.0 copy.16
  1.7 1.0 convert_element_type.33
  2.6 0.1 copy.17
  2.8 0.2 pad_maximum_fusion
  3.0 0.1 copy.18
  3.1 0.7 reshape.53.src
  3.8 15.5 %shard_map.86 = (bf16[32,16,128]{2,1,0:T(8,128)(2,1)}, bf16[2,4,256,128]{3,2,1,0:T(8,128)(2,1)}) custom-call(bf16[32,16,128]{2,1,0:T(8,128)(2,1)} %reshape.53.src, bf16[512,128]{1,0:T(8,128)(2,1)} %bitcast.37), custom_call_target="tpu_custom_call" | custom-call | tf_op jit(solution)/shard_map/pallas_call | solution.py:108
  19.3 1.2 %copy.19 = bf16[32,16,128]{0,2,1:T(8,128)(2,1)S(1)} copy(bf16[32,16,128]{2,1,0:T(8,128)(2,1)} %get-tuple-element.6) | data formatting | bytes 262144 | tf_op jit(solution)/shard_map/pallas_call | solution.py:108
  20.6 0.3 copy.21
  20.9 0.5 convert_element_type.35
  21.5 0.7 reshape.64.h_ref
  22.2 0.3 copy.20
  22.5 1.0 reshape_squeeze.3.x_ref
  23.5 19.9 %shard_map.87 = (bf16[2,128,128]{2,1,0:T(8,128)(2,1)}, bf16[4,4,2,512,128]{4,3,2,1,0:T(8,128)(2,1)}) custom-call(bf16[2,128,128]{2,1,0:T(8,128)(2,1)} %reshape_squeeze.3.x_ref, f32[2,1,16512]{2,1,0:T(1,128)} %reshape.64.h_ref, bf16[2,4,256,128]{3,2,1,0:T(8,128)(2,1)} %get-tuple-element.7.k_ref), custom_call_target="tpu_custom_call" | custom-call | tf_op jit(solution)/shard_map/pallas_call | solution.py:427
  43.4 1.2 %reshape.58 = bf16[2,32,32,16]{3,2,1,0:T(8,128)(2,1)S(1)} reshape(bf16[2,128,128]{2,1,0:T(8,128)(2,1)} %get-tuple-element.8) | data formatting | bytes 131072 | tf_op jit(solution)/shard_map/reshape | solution.py:669
  44.6 0.2 copy.22
  44.9 0.8 copy.23.src
  45.6 9.7 %shard_map.88 = bf16[32,8,128]{2,1,0:T(8,128)(2,1)} custom-call(bf16[32,8,128]{2,1,0:T(8,128)(2,1)} %copy.23.src), custom_call_target="tpu_custom_call" | custom-call | tf_op jit(solution)/shard_map/pallas_call | solution.py:90
  55.3 0.9 reshape.65
  56.2 0.1 copy.24
  56.3 0.7 fusion.m_ref
  57.1 43.3 %shard_map.89 = bf16[512,128]{1,0:T(8,128)(2,1)} custom-call(bf16[512,128]{1,0:T(8,128)(2,1)} %bitcast.34, bf16[4,4,2,512,128]{4,3,2,1,0:T(8,128)(2,1)} %get-tuple-element.9.k_far, bf16[64,512]{1,0:T(8,128)(2,1)} %fusion.m_ref, bf16[512,128]{1,0:T(8,128)(2,1)} %w_ref.1), custom_call_target="tpu_custom_call" | custom-call | tf_op jit(solution)/shard_map/pallas_call | solution.py:623
  100.4 0.8 copy.25
  101.1 1.6 %copy.27 = bf16[32,16,128]{2,1,0:T(8,128)(2,1)} copy(bf16[32,16,128]{2,1,0:T(8,128)(2,1)} %bitcast.32) | data formatting | bytes 262144
  (11 shorter events, 0.2 us)
Async XLA Ops:
  3.0 53.2 %copy-start.1 = (bf16[32,16,64]{2,1,0:T(8,128)(2,1)S(1)}, bf16[32,16,64]{2,1,0:T(8,128)(2,1)}, u32[]{:S(2)}) copy-start(bf16[32,16,64]{2,1,0:T(8,128)(2,1)} %param.8) | copy-start | bytes 196612
  19.3 37.0 %copy-start.2 = (f32[64]{0:T(128)S(1)}, f32[64]{0:T(128)}, u32[]{:S(2)}) copy-start(f32[64]{0:T(128)} %param.10) | copy-start | bytes 772
  57.1 43.3 %copy-start = (bf16[64,512]{1,0:T(8,128)(2,1)S(1)}, bf16[64,512]{1,0:T(8,128)(2,1)}, u32[]{:S(2)}) copy-start(bf16[64,512]{1,0:T(8,128)(2,1)} %fusion.m_ref) | copy-start | bytes 196612
